TPU v7x, 128 devices: a whole 4x4x4 slice. The times are simulated.
128 devices in a mesh: gx: 16 (over y, x_hi, core), gy: 8 (over z, x_lo).
Axes of the slice: x: 4 (x_hi: 2, x_lo: 2; x = x_hi * 2 + x_lo), y: 4, z: 4, core: 2. Of those that a mesh axis runs over, the one named last changes fastest.
Arguments:
- forces: float32 [3, 24, 32, 64, 128], P(None, None, 'gx', 'gy'), may hold values from -6 to 6
- levels: int32 [32, 64, 128], P('gx', 'gy'), may hold values from 0 to 15
- supports: int32 [32, 64, 128], P('gx', 'gy'), may hold values 0 or 1
Outputs:
- filtered: float32 [32, 64, 128], P('gx', 'gy')
All inputs are finite; a program needn't handle non-finite values. No bound on the sum of `supports` on one device may be relied on, other than what follows from the above.
Results may differ from a plain program's by a relative error of at most 0.0001.
Values sent between devices are 32-bit elements; how exact they have to be, the bound alone decides.
A program may use at most 128 MiB of HBM per device.

v0:
```python
import math

import jax
import jax.numpy as jnp
import numpy as np
from jax import lax
from jax.sharding import PartitionSpec as P

CASES = 24
LEVELS = 16
ITERS = 2


load_factor = 0.2


def from_behind(value, axis, steps):
    count = lax.axis_size(axis)
    leading, last = (max(0, -steps), min(count, count - steps))
    return lax.ppermute(value, axis, [(source, source + steps) for source in range(leading, last)])


def extended_2(x, sides, width):
    for axis, dim in sides:
        count, length = (lax.axis_size(axis), x.shape[dim])
        up = [(i, (i + 1) % count) for i in range(count - 1)]
        down = [(j, i) for i, j in up]
        last = lax.slice_in_dim(x, length - width, length, axis=dim)
        leading = lax.slice_in_dim(x, 0, width, axis=dim)
        before = lax.ppermute(last, axis, up)
        after = lax.ppermute(leading, axis, down)
        x = jnp.concatenate([before, x, after], axis=dim)
    return x


def element_matrix():
    poisson = 0.3
    lame_first = poisson / ((1.0 + poisson) * (1.0 - 2.0 * poisson))
    lame_shear = 1.0 / (2.0 * (1.0 + poisson))
    elastic = np.zeros((6, 6))
    elastic[:3, :3] = lame_first
    for position in range(3):
        elastic[position, position] += 2.0 * lame_shear
        elastic[position + 3, position + 3] = lame_shear
    points = [0.5 - 0.5 / math.sqrt(3.0), 0.5 + 0.5 / math.sqrt(3.0)]
    matrix = np.zeros((24, 24))
    for point_x in points:
        for point_y in points:
            for point_z in points:
                coords = (point_x, point_y, point_z)
                strain = np.zeros((6, 24))
                for corner in range(8):
                    corner_bits = (corner >> 2 & 1, corner >> 1 & 1, corner & 1)
                    shape_values = [
                        coords[axis_n] if corner_bits[axis_n] else 1.0 - coords[axis_n]
                        for axis_n in range(3)
                    ]
                    slopes = [1.0 if corner_bits[axis_n] else -1.0 for axis_n in range(3)]
                    slope_x = slopes[0] * shape_values[1] * shape_values[2]
                    slope_y = shape_values[0] * slopes[1] * shape_values[2]
                    slope_z = shape_values[0] * shape_values[1] * slopes[2]
                    offset = 3 * corner
                    strain[0, offset] = slope_x
                    strain[1, offset + 1] = slope_y
                    strain[2, offset + 2] = slope_z
                    strain[3, offset] = slope_y
                    strain[3, offset + 1] = slope_x
                    strain[4, offset + 1] = slope_z
                    strain[4, offset + 2] = slope_y
                    strain[5, offset] = slope_z
                    strain[5, offset + 2] = slope_x
                matrix = matrix + strain.T @ elastic @ strain / 8.0
    return matrix


def corner_stack(field_in, lead_in, span_x, span_y, span_z):
    pieces = []
    for corner in range(8):
        step_x, step_y, step_z = (corner >> 2 & 1, corner >> 1 & 1, corner & 1)
        pieces.append(
            field_in[
                :,
                :,
                lead_in + step_x : lead_in + step_x + span_x,
                lead_in + step_y : lead_in + step_y + span_y,
                lead_in + step_z : lead_in + step_z + span_z,
            ]
        )
    stacked = jnp.stack(pieces, 0)
    return stacked.reshape((24,) + stacked.shape[2:])


def element_forces(extended, stiff_ext, element_stiff):
    span_x, span_y, span_z = (extended.shape[2] - 2, extended.shape[3] - 2, extended.shape[4] - 2)
    outputs = []
    for first_case in range(0, extended.shape[1], 6):
        case_group = extended[:, first_case : first_case + 6]
        gathered = corner_stack(case_group, 0, span_x + 1, span_y + 1, span_z + 1)
        product = (
            jnp.einsum("ab,bcxyz->acxyz", element_stiff, gathered, precision=lax.Precision.HIGHEST)
            * stiff_ext
        )
        product = product.reshape((8, 3) + product.shape[1:])
        summed = jnp.zeros((3, case_group.shape[1], span_x, span_y, span_z), jnp.float32)
        for corner in range(8):
            step_x, step_y, step_z = (corner >> 2 & 1, corner >> 1 & 1, corner & 1)
            summed = (
                summed
                + product[corner][
                    :,
                    :,
                    1 - step_x : 1 - step_x + span_x,
                    1 - step_y : 1 - step_y + span_y,
                    1 - step_z : 1 - step_z + span_z,
                ]
            )
        outputs.append(summed)
    return jnp.concatenate(outputs, 1)


def element_energy(extended, element_stiff):
    span_x, span_y, span_z = (extended.shape[2] - 2, extended.shape[3] - 2, extended.shape[4] - 2)
    summed = jnp.zeros((span_x, span_y, span_z), jnp.float32)
    for first_case in range(0, extended.shape[1], 6):
        case_group = extended[:, first_case : first_case + 6]
        gathered = corner_stack(case_group, 1, span_x, span_y, span_z)
        product = jnp.einsum(
            "ab,bcxyz->acxyz", element_stiff, gathered, precision=lax.Precision.HIGHEST
        )
        summed = summed + jnp.sum(gathered * product, axis=(0, 1))
    return summed


def node_diagonal(stiff_ext, free_mask, element_stiff):
    span_x, span_y, span_z = free_mask.shape
    parts = []
    for component in range(3):
        summed = jnp.zeros((span_x, span_y, span_z), jnp.float32)
        for corner in range(8):
            step_x, step_y, step_z = (corner >> 2 & 1, corner >> 1 & 1, corner & 1)
            summed = (
                summed
                + stiff_ext[
                    1 - step_x : 1 - step_x + span_x,
                    1 - step_y : 1 - step_y + span_y,
                    1 - step_z : 1 - step_z + span_z,
                ]
                * element_stiff[3 * corner + component, 3 * corner + component]
            )
        parts.append(summed)
    diagonal = jnp.stack(parts, 0)[:, None]
    return 1.0 / (free_mask * diagonal + (1.0 - free_mask))


def block_gram(first_field, second_field):
    return jnp.einsum("kcxyz,kdxyz->cd", first_field, second_field, precision=lax.Precision.HIGHEST)


def combine(field_in, mixing):
    return jnp.einsum("kcxyz,cd->kdxyz", field_in, mixing, precision=lax.Precision.HIGHEST)


def cone_filter(rimmed, density):
    span_x, span_y, span_z = density.shape
    numerator = jnp.zeros((span_x, span_y, span_z), jnp.float32)
    denominator = jnp.zeros((span_x, span_y, span_z), jnp.float32)
    for shift_x in range(-2, 3):
        for shift_y in range(-2, 3):
            for shift_z in range(-2, 3):
                weight = 2.5 - math.sqrt(shift_x * shift_x + shift_y * shift_y + shift_z * shift_z)
                if weight > 0.0:
                    window = rimmed[
                        :,
                        2 + shift_x : 2 + shift_x + span_x,
                        2 + shift_y : 2 + shift_y + span_y,
                        2 + shift_z : 2 + shift_z + span_z,
                    ]
                    numerator = numerator + weight * window[0]
                    denominator = denominator + weight * window[1]
    return numerator / (density * denominator)


def local(forces, levels, supports):
    element_stiff = jnp.asarray(element_matrix(), jnp.float32)
    free_mask = (1 - supports).astype(jnp.float32)
    density = 0.3 + 0.7 * levels.astype(jnp.float32) / (LEVELS - 1)
    stiffness = density**3
    below_x = from_behind(stiffness[-1:], "gx", 1)
    widened = jnp.concatenate([below_x, stiffness], 0)
    below_y = from_behind(widened[:, -1:], "gy", 1)
    widened = jnp.concatenate([below_y, widened], 1)
    stiff_ext = jnp.pad(widened, ((0, 0), (0, 0), (1, 0)))
    inverse = node_diagonal(stiff_ext, free_mask, element_stiff)
    load_field = load_factor * free_mask * forces
    solution = jnp.zeros_like(load_field)
    residual = load_field
    direction = inverse * residual
    kept_rims = []
    alphas_kept = []
    for iteration in range(ITERS):
        extended = extended_2(free_mask * direction, (("gx", 2), ("gy", 3)), 1)
        extended = jnp.pad(extended, ((0, 0), (0, 0), (0, 0), (0, 0), (1, 1)))
        applied = (
            free_mask * element_forces(extended, stiff_ext, element_stiff)
            + (1.0 - free_mask) * direction
        )
        image_field, extended = (applied, extended)
        kept_rims.append(extended)
        curvature, along_dir = lax.psum(
            (block_gram(direction, image_field), block_gram(direction, residual)), ("gx", "gy")
        )
        factor = jnp.linalg.cholesky(curvature)
        step_alpha = jax.scipy.linalg.cho_solve((factor, True), along_dir)
        alphas_kept.append(step_alpha)
        solution = solution + combine(direction, step_alpha)
        residual = residual - combine(image_field, step_alpha)
        if iteration + 1 < ITERS:
            scaled_res = inverse * residual
            coupling = lax.psum(block_gram(image_field, scaled_res), ("gx", "gy"))
            step_beta = -jax.scipy.linalg.cho_solve((factor, True), coupling)
            direction = scaled_res + combine(direction, step_beta)
    masked_sol = free_mask * solution
    above_x = from_behind(masked_sol[:, :, :1], "gx", -1)
    sol_wide = jnp.concatenate([masked_sol, above_x], 2)
    above_y = from_behind(sol_wide[:, :, :, :1], "gy", -1)
    sol_wide = jnp.concatenate([sol_wide, above_y], 3)
    sol_ext = jnp.pad(sol_wide, ((0, 0), (0, 0), (1, 0), (1, 0), (1, 1)))
    energy = element_energy(sol_ext, element_stiff)
    sensitivity = -3.0 * density**2 * energy / CASES
    stacked = jnp.stack([density * sensitivity, jnp.ones_like(density)], 0)
    rimmed = extended_2(stacked, (("gx", 1), ("gy", 2)), 2)
    rimmed = jnp.pad(rimmed, ((0, 0), (0, 0), (0, 0), (2, 2)))
    return cone_filter(rimmed, density)


def solution(mesh):
    return jax.shard_map(
        local,
        mesh=mesh,
        in_specs=(P(None, None, "gx", "gy", None), P("gx", "gy", None), P("gx", "gy", None)),
        out_specs=P("gx", "gy", None),
        check_vma=False,
    )
```

profile of v0, /device:TPU:8, one launch (start us, length us, event | category | flops | bytes accessed | tf_op | source)
XLA Modules:
  0.0 547.2 jit_solution(6883320357306443744)
XLA Ops:
  2.6 5.4 collective-permute-done
  8.0 3.4 collective-permute-start.1
  17.1 6.0 %collective-permute-start.3 = (f32[3,24,1,8,128]{4,0,3,2,1:T(4,128)S(1)}, f32[3,24,1,8,128]{4,0,3,2,1:T(4,128)S(1)}, u32[]{:S(2)}, u32[]{:S(2)}) collective-permute-start(f32[3,24,1,8,128]{4,0,3,2,1:T(4,128)S(1)} %get-tuple-element.102), channel_id=1, source_target_pairs={{8,0},{16,8},{24,16},{32,24},{40,32},{48,40},{56,48},{64,56},{72,6... | collective-permute-start | bytes 884744 | tf_op jit(solution)/shard_map/ppermute | solution.py:31
  23.1 4.7 collective-permute-done.2
  28.5 4.2 collective-permute-start.4
  34.1 2.5 collective-permute-done.4
  36.6 7.4 %collective-permute-done.5 = f32[3,24,4,1,128]{4,0,3,2,1:T(4,128)S(1)} collective-permute-done((f32[3,24,4,1,128]{4,0,3,2,1:T(4,128)S(1)}, f32[3,24,4,1,128]{4,0,3,2,1:T(4,128)S(1)}, u32[]{:S(2)}, u32[]{:S(2)}) %collective-permute-start.5) | collective-permute-done | bytes 147488 | tf_op jit(solution)/shard_map/ppermute | solution.py:31
  44.0 4.2 select_maximum_fusion.4
  56.9 2.3 copy-done.3
  59.2 2.4 copy-done.5
  61.6 2.3 copy-done.6
  63.9 3.9 copy.32
  67.9 7.6 %reshape.547 = f32[24,6,3,9,129]{4,0,3,2,1:T(8,128)} reshape(f32[8,3,6,3,9,129]{5,1,0,4,3,2:T(4,128)} %copy.32) | data formatting | bytes 4012416 | tf_op jit(solution)/shard_map/reshape | solution.py:90
  75.4 2.4 fusion.46
  77.8 6.4 %copy.35 = f32[8,3,6,3,9,129]{5,1,0,4,3,2:T(4,128)} copy(f32[8,3,6,3,9,129]{5,1,4,3,2,0:T(4,128)} %fusion.46) | data formatting | bytes 4012416 | tf_op jit(solution)/shard_map/stack | solution.py:89
  84.2 7.4 %reshape.550 = f32[24,6,3,9,129]{4,0,3,2,1:T(8,128)} reshape(f32[8,3,6,3,9,129]{5,1,0,4,3,2:T(4,128)} %copy.35) | data formatting | bytes 4012416 | tf_op jit(solution)/shard_map/reshape | solution.py:90
  91.7 7.8 %multiply_bitcast_fusion.7 = f32[24,6,3,9,129]{4,0,3,2,1:T(8,128)} fusion(f32[24,6,3,9,129]{4,0,3,2,1:T(8,128)} %reshape.547, f32[24,24,1,1,1]{1,0,4,3,2:T(8,128)S(1)} %copy-done.11, f32[3,9,129]{2,1,0:T(8,128)S(1)} %pad.20), kind=kOutput, calls=%fused_computation.25 | convolution fusion | flops 144948528 | bytes 4028652 | tf_op jit(solution)/shard_map/ab,bcxyz->acxyz/dot_general | solution.py:100
  99.4 5.0 multiply_bitcast_fusion.4
  104.4 4.0 copy.34
  108.4 7.7 %reshape.549 = f32[24,6,3,9,129]{4,0,3,2,1:T(8,128)} reshape(f32[8,3,6,3,9,129]{5,1,0,4,3,2:T(4,128)} %copy.34) | data formatting | bytes 4012416 | tf_op jit(solution)/shard_map/reshape | solution.py:90
  116.1 7.6 %multiply_bitcast_fusion.5 = f32[24,6,3,9,129]{4,0,3,2,1:T(8,128)} fusion(f32[24,6,3,9,129]{4,0,3,2,1:T(8,128)} %reshape.549, f32[24,24,1,1,1]{1,0,4,3,2:T(8,128)S(1)} %copy-done.11, f32[3,9,129]{2,1,0:T(8,128)S(1)} %pad.20), kind=kOutput, calls=%fused_computation.23 | convolution fusion | flops 144948528 | bytes 4028652 | tf_op jit(solution)/shard_map/ab,bcxyz->acxyz/dot_general | solution.py:100
  123.7 6.5 %copy.33 = f32[8,3,6,3,9,129]{5,1,0,4,3,2:T(4,128)} copy(f32[8,3,6,3,9,129]{5,1,4,3,2,0:T(4,128)} %copy-done.6) | data formatting | bytes 4012416 | tf_op jit(solution)/shard_map/stack | solution.py:89
  130.2 7.4 %reshape.548 = f32[24,6,3,9,129]{4,0,3,2,1:T(8,128)} reshape(f32[8,3,6,3,9,129]{5,1,0,4,3,2:T(4,128)} %copy.33) | data formatting | bytes 4012416 | tf_op jit(solution)/shard_map/reshape | solution.py:90
  137.6 5.3 multiply_bitcast_fusion.6
  142.9 5.7 %slice_add_fusion.28 = (f32[3,6,2,8,128]{4,0,3,2,1:T(4,128)S(1)}, f32[3,6,2,8,128]{4,0,3,2,1:T(4,128)S(1)}) fusion(f32[24,6,3,9,129]{4,0,3,2,1:T(8,128)} %multiply_bitcast_fusion.4, f32[24,6,3,9,129]{4,0,3,2,1:T(8,128)} %multiply_bitcast_fusion.5), kind=kLoop, calls=%fused_computation.312 | loop fusion | flops 516096 | bytes 2654208 | tf_op jit(solution)/shard_map/add | solution.py:108
  148.6 4.0 slice_add_fusion.42
  156.1 67.5 %all-reduce.7 = (f32[24,24]{1,0:T(8,128)S(1)}, f32[24,24]{0,1:T(8,128)S(1)}) all-reduce(f32[24,24]{1,0:T(8,128)S(1)} %convolution_bitcast_fusion.5, f32[24,24]{0,1:T(8,128)S(1)} %convolution_bitcast_fusion.6), channel_id=1, replica_groups=mesh['gx'=16,'gy'=8] {'gx','gy'}, use_global_device_ids=true, to_apply=%region_3.5 | all-reduce | flops 1152 | bytes 9216 | tf_op jit(solution)/shard_map/psum | solution.py:209
  223.6 2.2 cholesky.44
  233.4 62.4 %psum.37 = f32[24,24]{1,0:T(8,128)S(1)} all-reduce(f32[24,24]{1,0:T(8,128)S(1)} %convolution_bitcast_fusion.3), channel_id=1, replica_groups=mesh['gx'=16,'gy'=8] {'gx','gy'}, use_global_device_ids=true, to_apply=%region_4.7 | all-reduce | flops 576 | bytes 4608 | tf_op jit(solution)/shard_map/psum | solution.py:219
  297.9 2.3 collective-permute-start.6
  300.2 6.0 %collective-permute-start.7 = (f32[3,24,1,8,128]{4,0,3,2,1:T(4,128)S(1)}, f32[3,24,1,8,128]{4,0,3,2,1:T(4,128)S(1)}, u32[]{:S(2)}, u32[]{:S(2)}) collective-permute-start(f32[3,24,1,8,128]{4,0,3,2,1:T(4,128)S(1)} %get-tuple-element.100), channel_id=1, source_target_pairs={{8,0},{16,8},{24,16},{32,24},{40,32},{48,40},{56,48},{64,56},{72,6... | collective-permute-start | bytes 884744 | tf_op jit(solution)/shard_map/ppermute | solution.py:31
  307.2 2.6 collective-permute-done.6
  311.7 3.2 collective-permute-start.8
  319.2 7.2 %collective-permute-done.9 = f32[3,24,4,1,128]{4,0,3,2,1:T(4,128)S(1)} collective-permute-done((f32[3,24,4,1,128]{4,0,3,2,1:T(4,128)S(1)}, f32[3,24,4,1,128]{4,0,3,2,1:T(4,128)S(1)}, u32[]{:S(2)}, u32[]{:S(2)}) %collective-permute-start.9) | collective-permute-done | bytes 147488 | tf_op jit(solution)/shard_map/ppermute | solution.py:31
  326.4 4.2 select_maximum_fusion
  339.3 2.3 copy-done.4
  341.6 2.4 copy-done.7
  344.0 2.3 copy-done.8
  346.4 3.9 copy.47
  350.3 7.4 %reshape.551 = f32[24,6,3,9,129]{4,0,3,2,1:T(8,128)} reshape(f32[8,3,6,3,9,129]{5,1,0,4,3,2:T(4,128)} %copy.47) | data formatting | bytes 4012416 | tf_op jit(solution)/shard_map/reshape | solution.py:90
  357.7 5.4 multiply_bitcast_fusion.3
  363.6 2.4 fusion.14
  366.0 6.4 %copy.50 = f32[8,3,6,3,9,129]{5,1,0,4,3,2:T(4,128)} copy(f32[8,3,6,3,9,129]{5,1,4,3,2,0:T(4,128)} %fusion.14) | data formatting | bytes 4012416 | tf_op jit(solution)/shard_map/stack | solution.py:89
  372.4 7.4 %reshape.554 = f32[24,6,3,9,129]{4,0,3,2,1:T(8,128)} reshape(f32[8,3,6,3,9,129]{5,1,0,4,3,2:T(4,128)} %copy.50) | data formatting | bytes 4012416 | tf_op jit(solution)/shard_map/reshape | solution.py:90
  379.8 5.3 multiply_bitcast_fusion
  385.6 6.4 %copy.49 = f32[8,3,6,3,9,129]{5,1,0,4,3,2:T(4,128)} copy(f32[8,3,6,3,9,129]{5,1,4,3,2,0:T(4,128)} %copy-done.7) | data formatting | bytes 4012416 | tf_op jit(solution)/shard_map/stack | solution.py:89
  392.0 7.4 %reshape.553 = f32[24,6,3,9,129]{4,0,3,2,1:T(8,128)} reshape(f32[8,3,6,3,9,129]{5,1,0,4,3,2:T(4,128)} %copy.49) | data formatting | bytes 4012416 | tf_op jit(solution)/shard_map/reshape | solution.py:90
  399.3 5.3 multiply_bitcast_fusion.1
  405.1 6.5 %copy.48 = f32[8,3,6,3,9,129]{5,1,0,4,3,2:T(4,128)} copy(f32[8,3,6,3,9,129]{5,1,4,3,2,0:T(4,128)} %copy-done.8) | data formatting | bytes 4012416 | tf_op jit(solution)/shard_map/stack | solution.py:89
  411.6 7.6 %reshape.552 = f32[24,6,3,9,129]{4,0,3,2,1:T(8,128)} reshape(f32[8,3,6,3,9,129]{5,1,0,4,3,2:T(4,128)} %copy.48) | data formatting | bytes 4012416 | tf_op jit(solution)/shard_map/reshape | solution.py:90
  419.2 5.3 multiply_bitcast_fusion.2
  426.6 64.6 %all-reduce.6 = (f32[24,24]{1,0:T(8,128)S(1)}, f32[24,24]{0,1:T(8,128)S(1)}) all-reduce(f32[24,24]{1,0:T(8,128)S(1)} %convolution_bitcast_fusion.1, f32[24,24]{0,1:T(8,128)S(1)} %convolution_bitcast_fusion.2), channel_id=1, replica_groups=mesh['gx'=16,'gy'=8] {'gx','gy'}, use_global_device_ids=true, to_apply=%region_6.9 | all-reduce | flops 1152 | bytes 9216 | tf_op jit(solution)/shard_map/psum | solution.py:209
  491.4 2.2 cholesky.55
  498.1 3.4 collective-permute-start.10
  501.5 4.2 collective-permute-done.10
  507.3 5.9 %collective-permute-done.11 = f32[3,24,3,1,128]{4,1,3,2,0:T(8,128)S(1)} collective-permute-done((f32[3,24,3,1,128]{4,1,3,2,0:T(8,128)S(1)}, f32[3,24,3,1,128]{4,1,3,2,0:T(8,128)S(1)}, u32[]{:S(2)}, u32[]{:S(2)}) %collective-permute-start.11) | collective-permute-done | bytes 110624 | tf_op jit(solution)/shard_map/ppermute | solution.py:20
  514.2 2.3 fusion.2
  516.9 2.3 fusion.1
  519.6 2.3 fusion.3
  522.1 2.3 fusion.4
  524.4 4.2 collective-permute-start.13
  530.6 5.5 %collective-permute-done.12 = f32[2,2,8,128]{3,2,1,0:T(8,128)S(1)} collective-permute-done((f32[2,2,8,128]{3,2,1,0:T(8,128)S(1)}, f32[2,2,8,128]{3,2,1,0:T(8,128)S(1)}, u32[]{:S(2)}, u32[]{:S(2)}) %collective-permute-start.12) | collective-permute-done | bytes 16416 | tf_op jit(solution)/shard_map/ppermute | solution.py:30
  536.1 3.9 collective-permute-start.14
  541.5 4.2 collective-permute-done.15
  (128 shorter events, 63.8 us)
Async XLA Ops:
  0.7 7.3 %collective-permute-start = (f32[1,8,128]{2,1,0:T(8,128)S(1)}, f32[1,8,128]{2,1,0:T(8,128)S(1)}, u32[]{:S(2)}, u32[]{:S(2)}) collective-permute-start(f32[1,8,128]{2,1,0:T(8,128)S(1)} %slice.2141), channel_id=1, source_target_pairs={{0,8},{8,16},{16,24},{24,32},{32,40},{40,48},{48,56},{56,64},{64,7... | collective-permute-start | bytes 12296 | tf_op jit(solution)/shard_map/ppermute | solution.py:20
  8.0 4.7 collective-permute-start.1
  15.1 12.7 %collective-permute-start.2 = (f32[3,24,1,8,128]{4,0,3,2,1:T(4,128)S(1)}, f32[3,24,1,8,128]{4,0,3,2,1:T(4,128)S(1)}, u32[]{:S(2)}, u32[]{:S(2)}) collective-permute-start(f32[3,24,1,8,128]{4,0,3,2,1:T(4,128)S(1)} %get-tuple-element.101), channel_id=1, source_target_pairs={{0,8},{8,16},{16,24},{24,32},{32,40},{40,48},{48,56},{56,64},{64,7... | collective-permute-start | bytes 884744 | tf_op jit(solution)/shard_map/ppermute | solution.py:30
  17.1 11.3 %collective-permute-start.3 = (f32[3,24,1,8,128]{4,0,3,2,1:T(4,128)S(1)}, f32[3,24,1,8,128]{4,0,3,2,1:T(4,128)S(1)}, u32[]{:S(2)}, u32[]{:S(2)}) collective-permute-start(f32[3,24,1,8,128]{4,0,3,2,1:T(4,128)S(1)} %get-tuple-element.102), channel_id=1, source_target_pairs={{8,0},{16,8},{24,16},{32,24},{40,32},{48,40},{56,48},{64,56},{72,6... | collective-permute-start | bytes 884744 | tf_op jit(solution)/shard_map/ppermute | solution.py:31
  28.5 8.1 %collective-permute-start.4 = (f32[3,24,4,1,128]{4,0,3,2,1:T(4,128)S(1)}, f32[3,24,4,1,128]{4,0,3,2,1:T(4,128)S(1)}, u32[]{:S(2)}, u32[]{:S(2)}) collective-permute-start(f32[3,24,4,1,128]{4,0,3,2,1:T(4,128)S(1)} %get-tuple-element.79), channel_id=1, source_target_pairs={{0,1},{1,2},{2,3},{3,4},{4,5},{5,6},{6,7},{8,9},{9,10},{10,11},{11... | collective-permute-start | bytes 442376 | tf_op jit(solution)/shard_map/ppermute | solution.py:30
  32.7 11.3 %collective-permute-start.5 = (f32[3,24,4,1,128]{4,0,3,2,1:T(4,128)S(1)}, f32[3,24,4,1,128]{4,0,3,2,1:T(4,128)S(1)}, u32[]{:S(2)}, u32[]{:S(2)}) collective-permute-start(f32[3,24,4,1,128]{4,0,3,2,1:T(4,128)S(1)} %get-tuple-element.80), channel_id=1, source_target_pairs={{1,0},{2,1},{3,2},{4,3},{5,4},{6,5},{7,6},{9,8},{10,9},{11,10},{12... | collective-permute-start | bytes 442376 | tf_op jit(solution)/shard_map/ppermute | solution.py:31
  48.2 7.3 %copy-start.1 = (f32[3,24,4,10,130]{4,0,3,2,1:T(4,128)}, f32[3,24,4,10,130]{4,0,3,2,1:T(4,128)S(1)}, u32[]{:S(2)}) copy-start(f32[3,24,4,10,130]{4,0,3,2,1:T(4,128)S(1)} %select_maximum_fusion.4) | copy-start | bytes 4492804
  56.9 2.3 copy-start.3
  59.2 2.4 copy-start.5
  61.6 2.3 copy-start.6
  84.2 7.4 %copy-start.11 = (f32[24,24,1,1,1]{1,0,4,3,2:T(8,128)S(1)}, f32[24,24,1,1,1]{1,0,4,3,2:T(8,128)}, u32[]{:S(2)}) copy-start(f32[24,24,1,1,1]{1,0,4,3,2:T(8,128)} %constant.139) | copy-start | bytes 6916
  91.6 7.8 %copy-start.2 = (f32[24,6,3,9,129]{4,0,3,2,1:T(8,128)S(1)}, f32[24,6,3,9,129]{4,0,3,2,1:T(8,128)}, u32[]{:S(2)}) copy-start(f32[24,6,3,9,129]{4,0,3,2,1:T(8,128)} %reshape.550) | copy-start | bytes 6018628
  91.6 12.8 %slice-start = ((s8[5308416]{0:T(1024)(128)(4,1)}), s8[4194304]{0:T(1024)(128)(4,1)S(1)}, s32[]{:S(2)}) async-start(s8[5308416]{0:T(1024)(128)(4,1)} %bitcast.1302), calls=%async_computation | async-start | bytes 8388608
  99.4 5.0 slice-start.1
  142.9 9.7 %copy-start.9 = (f32[3,24,2,8,128]{4,3,2,1,0:T(8,128)S(1)}, f32[3,24,2,8,128]{4,3,2,1,0:T(8,128)}, u32[]{:S(2)}) copy-start(f32[3,24,2,8,128]{4,3,2,1,0:T(8,128)} %param.7) | copy-start | bytes 1769476
  297.1 19.0 %copy-start.10 = (f32[3,24,2,8,128]{4,0,3,2,1:T(4,128)S(1)}, f32[3,24,2,8,128]{4,0,3,2,1:T(4,128)}, u32[]{:S(2)}) copy-start(f32[3,24,2,8,128]{4,0,3,2,1:T(4,128)} %get-tuple-element.14) | copy-start | bytes 1769476
  297.9 11.9 %collective-permute-start.6 = (f32[3,24,1,8,128]{4,0,3,2,1:T(4,128)S(1)}, f32[3,24,1,8,128]{4,0,3,2,1:T(4,128)S(1)}, u32[]{:S(2)}, u32[]{:S(2)}) collective-permute-start(f32[3,24,1,8,128]{4,0,3,2,1:T(4,128)S(1)} %get-tuple-element.99), channel_id=1, source_target_pairs={{0,8},{8,16},{16,24},{24,32},{32,40},{40,48},{48,56},{56,64},{64,7... | collective-permute-start | bytes 884744 | tf_op jit(solution)/shard_map/ppermute | solution.py:30
  300.2 11.3 %collective-permute-start.7 = (f32[3,24,1,8,128]{4,0,3,2,1:T(4,128)S(1)}, f32[3,24,1,8,128]{4,0,3,2,1:T(4,128)S(1)}, u32[]{:S(2)}, u32[]{:S(2)}) collective-permute-start(f32[3,24,1,8,128]{4,0,3,2,1:T(4,128)S(1)} %get-tuple-element.100), channel_id=1, source_target_pairs={{8,0},{16,8},{24,16},{32,24},{40,32},{48,40},{56,48},{64,56},{72,6... | collective-permute-start | bytes 884744 | tf_op jit(solution)/shard_map/ppermute | solution.py:31
  311.7 7.5 %collective-permute-start.8 = (f32[3,24,4,1,128]{4,0,3,2,1:T(4,128)S(1)}, f32[3,24,4,1,128]{4,0,3,2,1:T(4,128)S(1)}, u32[]{:S(2)}, u32[]{:S(2)}) collective-permute-start(f32[3,24,4,1,128]{4,0,3,2,1:T(4,128)S(1)} %get-tuple-element.77), channel_id=1, source_target_pairs={{0,1},{1,2},{2,3},{3,4},{4,5},{5,6},{6,7},{8,9},{9,10},{10,11},{11... | collective-permute-start | bytes 442376 | tf_op jit(solution)/shard_map/ppermute | solution.py:30
  314.8 11.6 %collective-permute-start.9 = (f32[3,24,4,1,128]{4,0,3,2,1:T(4,128)S(1)}, f32[3,24,4,1,128]{4,0,3,2,1:T(4,128)S(1)}, u32[]{:S(2)}, u32[]{:S(2)}) collective-permute-start(f32[3,24,4,1,128]{4,0,3,2,1:T(4,128)S(1)} %get-tuple-element.78), channel_id=1, source_target_pairs={{1,0},{2,1},{3,2},{4,3},{5,4},{6,5},{7,6},{9,8},{10,9},{11,10},{12... | collective-permute-start | bytes 442376 | tf_op jit(solution)/shard_map/ppermute | solution.py:31
  330.6 7.3 %copy-start = (f32[3,24,4,10,130]{4,0,3,2,1:T(4,128)}, f32[3,24,4,10,130]{4,0,3,2,1:T(4,128)S(1)}, u32[]{:S(2)}) copy-start(f32[3,24,4,10,130]{4,0,3,2,1:T(4,128)S(1)} %select_maximum_fusion) | copy-start | bytes 4492804
  339.3 2.3 copy-start.4
  341.6 2.4 copy-start.7
  344.0 2.3 copy-start.8
  498.1 7.6 %collective-permute-start.10 = (f32[3,24,1,8,128]{4,1,3,2,0:T(8,128)S(1)}, f32[3,24,1,8,128]{4,1,3,2,0:T(8,128)S(1)}, u32[]{:S(2)}, u32[]{:S(2)}) collective-permute-start(f32[3,24,1,8,128]{4,1,3,2,0:T(8,128)S(1)} %slice.2277), channel_id=1, source_target_pairs={{8,0},{16,8},{24,16},{32,24},{40,32},{48,40},{56,48},{64,56},{72,6... | collective-permute-start | bytes 884744 | tf_op jit(solution)/shard_map/ppermute | solution.py:20
  505.8 7.5 %collective-permute-start.11 = (f32[3,24,3,1,128]{4,1,3,2,0:T(8,128)S(1)}, f32[3,24,3,1,128]{4,1,3,2,0:T(8,128)S(1)}, u32[]{:S(2)}, u32[]{:S(2)}) collective-permute-start(f32[3,24,3,1,128]{4,1,3,2,0:T(8,128)S(1)} %pad_maximum_fusion.8), channel_id=1, source_target_pairs={{1,0},{2,1},{3,2},{4,3},{5,4},{6,5},{7,6},{9,8},{10,9},{11,10},{12... | collective-permute-start | bytes 331784 | tf_op jit(solution)/shard_map/ppermute | solution.py:20
  519.2 5.1 copy-start.12
  524.4 6.2 %collective-permute-start.13 = (f32[2,2,8,128]{3,2,1,0:T(8,128)S(1)}, f32[2,2,8,128]{3,2,1,0:T(8,128)S(1)}, u32[]{:S(2)}, u32[]{:S(2)}) collective-permute-start(f32[2,2,8,128]{3,2,1,0:T(8,128)S(1)} %stack.455), channel_id=1, source_target_pairs={{8,0},{16,8},{24,16},{32,24},{40,32},{48,40},{56,48},{64,56},{72,6... | collective-permute-start | bytes 49160 | tf_op jit(solution)/shard_map/ppermute | solution.py:31
  528.7 7.5 %collective-permute-start.12 = (f32[2,2,8,128]{3,2,1,0:T(8,128)S(1)}, f32[2,2,8,128]{3,2,1,0:T(8,128)S(1)}, u32[]{:S(2)}, u32[]{:S(2)}) collective-permute-start(f32[2,2,8,128]{3,2,1,0:T(8,128)S(1)} %stack.455), channel_id=1, source_target_pairs={{0,8},{8,16},{16,24},{24,32},{32,40},{40,48},{48,56},{56,64},{64,7... | collective-permute-start | bytes 49160 | tf_op jit(solution)/shard_map/ppermute | solution.py:30
  536.1 5.3 collective-permute-start.14
  540.1 5.6 %collective-permute-start.15 = (f32[2,6,2,128]{3,2,1,0:T(2,128)S(1)}, f32[2,6,2,128]{3,2,1,0:T(2,128)S(1)}, u32[]{:S(2)}, u32[]{:S(2)}) collective-permute-start(f32[2,6,2,128]{3,2,1,0:T(2,128)S(1)} %get-tuple-element.113), channel_id=1, source_target_pairs={{1,0},{2,1},{3,2},{4,3},{5,4},{6,5},{7,6},{9,8},{10,9},{11,10},{12... | collective-permute-start | bytes 36872 | tf_op jit(solution)/shard_map/ppermute | solution.py:31
where the time goes:
time: 558 us; the launch traced here: 547 us
  blocking collectives  195 us (35%)
  local copies, waits for them, and re-layouts  142 us (25%)
  matrix products  67.7 us (12%)
  waiting for transfers between devices  54.4 us (10%)
  starting transfers between devices  47.9 us (9%)
  other arithmetic  39.2 us (7%)
    psum x2, blocking collectives, local(): lax.psum((block_gram(direction, image_field), block_gram(direction, resid...  132 us
    psum x1, blocking collectives, local(): coupling = lax.psum(block_gram(image_field, scaled_res), ('gx', 'gy'))  62.4 us
    reshape x8, local copies, waits for them, and re-layouts, corner_stack(): return stacked.reshape((24,) + stacked.shape[2:])  59.9 us
    another operation x16, local copies, waits for them, and re-layouts, corner_stack(): stacked = jnp.stack(pieces, 0)  52.4 us
    dot_general x8, matrix products, element_forces(): jnp.einsum('ab,bcxyz->acxyz', element_stiff, gathered, precision=lax.Prec...  46.9 us
    unnamed x55, local copies, waits for them, and re-layouts  29.4 us
    ppermute x6, waiting for transfers between devices, extended_2(): after = lax.ppermute(leading, axis, down)  21.1 us
    ppermute x6, starting transfers between devices, extended_2(): after = lax.ppermute(leading, axis, down)  20.2 us
  transfers between devices with their start and end apart: 16, of which 15 were waited for; matrix products, arithmetic and copies ran while one was open for 1% of the time, Pallas kernels for 0%

commit v1 on v0

v1 whole, which is shorter than its diff:
```python
import functools
import math

import jax
import jax.numpy as jnp
import numpy as np
from jax import lax
from jax.experimental import pallas as pl
from jax.experimental.pallas import tpu as pltpu
from jax.sharding import PartitionSpec as P

MESH = pl.DeviceIdType.MESH
CASES = 24
LEVELS = 16
LOAD = 0.2
BX, BY, NZ = 2, 8, 128
CT = 3


def element_matrix():
    poisson = 0.3
    lame_first = poisson / ((1.0 + poisson) * (1.0 - 2.0 * poisson))
    lame_shear = 1.0 / (2.0 * (1.0 + poisson))
    elastic = np.zeros((6, 6))
    elastic[:3, :3] = lame_first
    for position in range(3):
        elastic[position, position] += 2.0 * lame_shear
        elastic[position + 3, position + 3] = lame_shear
    points = [0.5 - 0.5 / math.sqrt(3.0), 0.5 + 0.5 / math.sqrt(3.0)]
    matrix = np.zeros((24, 24))
    for point_x in points:
        for point_y in points:
            for point_z in points:
                coords = (point_x, point_y, point_z)
                strain = np.zeros((6, 24))
                for corner in range(8):
                    bits = (corner >> 2 & 1, corner >> 1 & 1, corner & 1)
                    shape = [coords[n] if bits[n] else 1.0 - coords[n] for n in range(3)]
                    slopes = [1.0 if bits[n] else -1.0 for n in range(3)]
                    slope_x = slopes[0] * shape[1] * shape[2]
                    slope_y = shape[0] * slopes[1] * shape[2]
                    slope_z = shape[0] * shape[1] * slopes[2]
                    o = 3 * corner
                    strain[0, o] = slope_x
                    strain[1, o + 1] = slope_y
                    strain[2, o + 2] = slope_z
                    strain[3, o] = slope_y
                    strain[3, o + 1] = slope_x
                    strain[4, o + 1] = slope_z
                    strain[4, o + 2] = slope_y
                    strain[5, o] = slope_z
                    strain[5, o + 2] = slope_x
                matrix = matrix + strain.T @ elastic @ strain / 8.0
    return matrix


KE = element_matrix()
DIAG = float(KE[0, 0])


def parity_matrix():
    walsh = np.ones((8, 8))
    for mode in range(8):
        for corner in range(8):
            for n in range(3):
                if mode >> n & 1:
                    walsh[mode, corner] *= 2 * (corner >> n & 1) - 1
    big = np.kron(walsh, np.eye(3))
    return big @ KE @ big.T / 64.0


KP = parity_matrix()
UNIT = ((1, 0, 0), (0, 1, 0), (0, 0, 1))


def _flip(p, k):
    return tuple(a ^ b for a, b in zip(p, UNIT[k]))


def _kp(m, n):
    at = [3 * (4 * p[0] + 2 * p[1] + p[2]) + k for k, p in (m, n)]
    return float(KP[at[0], at[1]])


NORMAL = [(k, UNIT[k]) for k in range(3)]
BEND = [(k, _flip((1, 1, 1), k)) for k in range(3)]
PAIRS = [[(k, _flip(UNIT[s], k)) for k in range(3) if k != s] for s in range(3)]
SHEAR = []
TWIST = []
for _s in range(3):
    _a, _b = [k for k in range(3) if k != _s]
    SHEAR.append([(_a, UNIT[_b]), (_b, UNIT[_a])])
    TWIST.append((_s, (1, 1, 1)))
N_OFF = _kp(NORMAL[0], NORMAL[1])
N_DIA = _kp(NORMAL[0], NORMAL[0]) - N_OFF
P_OFF = _kp(PAIRS[0][0], PAIRS[0][1])
P_DIA = _kp(PAIRS[0][0], PAIRS[0][0]) - P_OFF
S_ALL = _kp(SHEAR[0][0], SHEAR[0][0])
T_ALL = _kp(TWIST[0], TWIST[0])
B_OFF = _kp(BEND[0], BEND[1])
B_DIA = _kp(BEND[0], BEND[0]) - B_OFF


def _span(d, low, high, size):
    a = max(0, low + d * size)
    b = min(size, high + 1 + d * size)
    return a, a - d * size, b - a


NEIGHBOURS = [(dx, dy) for dx in (-1, 0, 1) for dy in (-1, 0, 1) if dx or dy]


def _shift(x, by):
    lane = lax.broadcasted_iota(jnp.int32, x.shape, x.ndim - 1)
    r = pltpu.roll(x, (-by) % NZ, axis=x.ndim - 1)
    ok = lane < NZ - by if by > 0 else lane >= -by
    return jnp.where(ok, r, 0.0)


def _stage(u_at, ex, y, ct):
    out = {}
    for k in range(3):
        u0, u1 = u_at(k, ex, y, ct), u_at(k, ex + 1, y, ct)
        for px, b in ((0, u0 + u1), (1, u1 - u0)):
            up = _shift(b, 1)
            out[k, px, 0] = b + up
            out[k, px, 1] = up - b
    return out


KEYS = [(k, px, pz) for k in range(3) for px in (0, 1) for pz in (0, 1)]


def _modes(s0, s1):
    out = {}
    for k, px, pz in KEYS:
        if (px, pz) != (0, 0):
            out[k, (px, 0, pz)] = s0[k, px, pz] + s1[k, px, pz]
        out[k, (px, 1, pz)] = s1[k, px, pz] - s0[k, px, pz]
    return out


def _stress(u, e):
    g = {}
    total = (u[NORMAL[0]] + u[NORMAL[1]] + u[NORMAL[2]]) * (e * N_OFF)
    dia = e * N_DIA
    for m in NORMAL:
        g[m] = u[m] * dia + total
    total = u[BEND[0]] + u[BEND[1]] + u[BEND[2]]
    total = total * (e * B_OFF)
    dia = e * B_DIA
    for m in BEND:
        g[m] = u[m] * dia + total
    off, dia = e * P_OFF, e * P_DIA
    for a, b in PAIRS:
        total = (u[a] + u[b]) * off
        g[a] = u[a] * dia + total
        g[b] = u[b] * dia + total
    both = e * S_ALL
    for a, b in SHEAR:
        g[a] = g[b] = (u[a] + u[b]) * both
    alone = e * T_ALL
    for m in TWIST:
        g[m] = u[m] * alone
    return g


def _density_of_energy(u):
    def sq(x):
        return x * x

    e = N_OFF * sq(u[NORMAL[0]] + u[NORMAL[1]] + u[NORMAL[2]])
    e = e + N_DIA * (sq(u[NORMAL[0]]) + sq(u[NORMAL[1]]) + sq(u[NORMAL[2]]))
    e = e + B_OFF * sq(u[BEND[0]] + u[BEND[1]] + u[BEND[2]])
    e = e + B_DIA * (sq(u[BEND[0]]) + sq(u[BEND[1]]) + sq(u[BEND[2]]))
    off = dia = she = twi = 0.0
    for a, b in PAIRS:
        off = off + sq(u[a] + u[b])
        dia = dia + sq(u[a]) + sq(u[b])
    for a, b in SHEAR:
        she = she + sq(u[a] + u[b])
    for m in TWIST:
        twi = twi + sq(u[m])
    return e + P_OFF * off + P_DIA * dia + S_ALL * she + T_ALL * twi


def _apply(u_at, e_at, add, layers, y_low, columns, close, unroll=2):
    def tile(ct, _):
        for ex in layers:
            first = _stage(u_at, ex, y_low, ct)
            zero = jnp.zeros((8, NZ), jnp.float32)

            def emit(y, h, ex=ex):
                for k in range(3):
                    p = []
                    for px in (0, 1):
                        s, d = h[k, px, 0], h[k, px, 1]
                        p.append((s - d) + _shift(s + d, -1))
                    add(k, ex, ex, y, ct, p[0] - p[1])
                    add(k, ex, ex + 1, y, ct, p[0] + p[1])

            def step(t, state, ex=ex):
                s0 = dict(zip(KEYS, state[0]))
                carry = dict(zip(KEYS, state[1]))
                y = y_low + t
                s1 = _stage(u_at, ex, y + 1, ct)
                g = _stress(_modes(s0, s1), e_at(ex, y))
                h, later = {}, {}
                for key in KEYS:
                    k, px, pz = key
                    g1 = g[k, (px, 1, pz)]
                    g0 = g.get((k, (px, 0, pz)))
                    if g0 is None:
                        h[key] = carry[key] - g1
                        later[key] = g1
                    else:
                        h[key] = carry[key] + (g0 - g1)
                        later[key] = g0 + g1
                emit(y, h)
                return tuple(s1[key] for key in KEYS), tuple(later[key] for key in KEYS)

            state = (tuple(first[key] for key in KEYS), (zero,) * len(KEYS))
            state = lax.fori_loop(0, columns, step, state, unroll=unroll)
            if close:
                emit(y_low + columns, dict(zip(KEYS, state[1])))
        return 0

    lax.fori_loop(0, CT, tile, 0)


def _split(x):
    scaled = x * 65537.0
    high = scaled - (scaled - x)
    return high.astype(jnp.bfloat16), (x - high).astype(jnp.bfloat16)


def _rows(x):
    return x.reshape(CASES, NZ)


def _nt(a, b):
    return lax.dot_general(a, b, (((1,), (1,)), ((), ())), preferred_element_type=jnp.float32)


def _solve(table):
    lane = lax.broadcasted_iota(jnp.int32, (CASES, NZ), 1)

    def left(x, by):
        return pltpu.roll(x, (-by) % NZ, axis=1)

    def join(a, b):
        return jnp.where(lane < 24, a, jnp.where(lane < 48, b, 0.0))

    blocks = [
        join(table, left(table, 24)),
        join(left(table, 48), left(table, 72)),
        join(left(table, 24), left(table, 48)),
    ]
    tiles = [b[8 * i : 8 * i + 8] for b in blocks for i in range(3)]
    lane8 = lax.broadcasted_iota(jnp.int32, (1, NZ), 1)
    scales = jnp.zeros((1, NZ), jnp.float32)
    for j in range(48):
        own = tiles[j // 8]
        row = own[j % 8 : j % 8 + 1]
        pivot = row[:, j : j + 1]
        scale = 1.0 / pivot
        factor = jnp.where(lane8 == j, 0.0, row * scale)
        scales = jnp.where(lane8 == j, scale, scales)
        live = range((j + 1) // 8, 9)
        for t in live:
            tiles[t] = tiles[t] - tiles[t][:, j : j + 1] * factor
    return jnp.concatenate(tiles[6:], 0) * scales


WEIGHT = {}
for _dx in range(-2, 3):
    for _dy in range(-2, 3):
        for _dz in range(3):
            _w = 2.5 - math.sqrt(_dx * _dx + _dy * _dy + _dz * _dz)
            if _w > 0.0:
                WEIGHT[_dx, _dy, _dz] = _w


def _cone(planes):
    result = []
    for xo in range(BX):
        total = jnp.zeros((BY, NZ), jnp.float32)
        for (dx, dy, dz), w in WEIGHT.items():
            total = total + w * planes(xo + 2 + dx, dy, dz)
        result.append(total)
    return result


def _kernel(nx, ny, phases, forces, levels, supports, out, nat, lev, sup, stiff, stiffz, inv, free, field, dire, masked,
            image, qf, qm, wf, split, disp, energy, vals, zsum, gram_send, gram_recv, local_sem, l_send, l_recv, s_send,
            s_recv, f_send, f_recv, v_send, v_recv, g_send, g_recv):
    i, j = lax.axis_index("gx"), lax.axis_index("gy")

    def there(dx, dy):
        return lax.rem(i + dx + nx, nx), lax.rem(j + dy + ny, ny)

    peers = [there(dx, dy) for dx, dy in NEIGHBOURS]
    for phase in phases:
        for ox, oy in phase:
            peers.append((i ^ ox, j ^ oy))

    c_nat = pltpu.make_async_copy(forces, nat, local_sem.at[0])
    c_lev = pltpu.make_async_copy(levels, lev.at[2 : 2 + BX, 2 : 2 + BY], local_sem.at[1])
    c_sup = pltpu.make_async_copy(supports, sup.at[1 : 1 + BX, 1 : 1 + BY], local_sem.at[2])
    c_nat.start()
    c_lev.start()
    c_sup.start()

    barrier = pltpu.get_barrier_semaphore()
    for peer in peers:
        pl.semaphore_signal(barrier, inc=1, device_id=peer, device_id_type=MESH)

    c_nat.wait()

    def arrange(t, _):
        k = t // (BX * BY)
        x = (t // BY) % BX
        y = t % BY
        rows = nat[pl.ds(k * (CASES * BX * BY) + x * BY + y, CASES, stride=BX * BY), :]
        field[k, 1 + x, 1 + y] = rows.reshape(CT, 8, NZ)
        return 0

    lax.fori_loop(0, 3 * BX * BY, arrange, 0, unroll=4)
    c_lev.wait()
    c_sup.wait()

    pl.semaphore_wait(barrier, len(peers))

    copies = []
    for n, (dx, dy) in enumerate(NEIGHBOURS):
        peer = there(dx, dy)
        (a, b, c), (d, e, f) = _span(dx, -2, 3, BX), _span(dy, -2, 9, BY)
        copies.append(pltpu.make_async_remote_copy(
            levels.at[a : a + c, d : d + f], lev.at[b + 2 : b + 2 + c, e + 2 : e + 2 + f],
            l_send.at[n], l_recv.at[n], device_id=peer, device_id_type=MESH))
        (a, b, c), (d, e, f) = _span(dx, -1, 3, BX), _span(dy, -1, 9, BY)
        copies.append(pltpu.make_async_remote_copy(
            supports.at[a : a + c, d : d + f], sup.at[b + 1 : b + 1 + c, e + 1 : e + 1 + f],
            s_send.at[n], s_recv.at[n], device_id=peer, device_id_type=MESH))
        copies.append(pltpu.make_async_remote_copy(
            field.at[:, a + 1 : a + 1 + c, d + 1 : d + 1 + f], field.at[:, b + 1 : b + 1 + c, e + 1 : e + 1 + f],
            f_send.at[n], f_recv.at[n], device_id=peer, device_id_type=MESH))
    for n in (0, 1):
        for copy in copies[n::3]:
            copy.start()
    for copy in copies[2::3]:
        copy.start()
    for n in (0, 1):
        for copy in copies[n::3]:
            copy.wait()

    def inside(x, y):
        gx, gy = i * BX + x, j * BY + y
        ok = (gx >= 0) & (gx < nx * BX) & (gy >= 0) & (gy < ny * BY)
        return jnp.where(ok, 1.0, 0.0).astype(jnp.float32)

    def moduli(t, _):
        x, y = t // (BY + 4), t % (BY + 4)
        level = jnp.broadcast_to(lev[x, y], (8, NZ)).astype(jnp.float32)
        rho = 0.3 + 0.7 * level / (LEVELS - 1)
        e = rho * rho * rho * inside(x - 2, y - 2)
        stiff[x, y] = e
        stiffz[x, y] = e + _shift(e, -1)
        return 0

    lax.fori_loop(0, (BX + 4) * (BY + 4), moduli, 0, unroll=2)

    def nodal(t, _):
        x, y = t // (BY + 3), t % (BY + 3)
        fr = (1 - jnp.broadcast_to(sup[x, y], (8, NZ))).astype(jnp.float32) * inside(x - 1, y - 1)
        total = stiffz[x, y] + stiffz[x + 1, y] + stiffz[x, y + 1] + stiffz[x + 1, y + 1]
        free[x, y] = fr
        inv[x, y] = 1.0 / (fr * (DIAG * total) + (1.0 - fr))
        return 0

    lax.fori_loop(0, (BX + 3) * (BY + 3), nodal, 0, unroll=2)

    for copy in copies[2::3]:
        copy.wait()

    def search(t, _):
        x, y = t // (BY + 3), t % (BY + 3)
        fr, iv = free[x, y], inv[x, y]
        for k in range(3):
            d = iv * (LOAD * fr * field[k, x, y])
            dire[k, x, y] = d
            masked[k, x, y] = fr * d
        return 0

    lax.fori_loop(0, (BX + 3) * (BY + 3), search, 0)

    def u_at(k, x, y, ct):
        return masked[k, x + 1, y + 1, ct]

    def e_at(x, y):
        return stiff[x + 2, y + 2]

    def add_image(k, ex, x, y, ct, value):
        if x < 0 or x > BX:
            return
        if x == ex:
            image[k, x, y + 1, ct] += value
        else:
            image[k, x, y + 1, ct] = value

    _apply(u_at, e_at, add_image, range(-1, BX + 1), -1, BY + 2, False)

    def above(x, y):
        fr, iv = free[x + 1, y + 1], inv[x + 1, y + 1]
        out = []
        for k in range(3):
            d = dire[k, x + 1, y + 1]
            im = fr * image[k, x, y + 1] + (1.0 - fr) * d
            q = iv * im
            qf[k, x, y] = q
            qm[k, x, y] = fr * q
            both = jnp.concatenate([_rows(d), _rows(q)], 0)
            high, low = _split(both)
            hl = jnp.concatenate([high, low], 0)
            split[k, x, y] = hl
            out.append((hl, im, fr))
        return out

    gap = jnp.zeros((16, NZ), jnp.bfloat16)

    def first_gram(t, acc):
        x, y = t // BY, t % BY
        for k, (hl, im, fr) in enumerate(above(x, y)):
            r0 = LOAD * fr * field[k, x + 1, y + 1]
            high, low = _split(jnp.concatenate([_rows(im), _rows(r0)], 0))
            acc = acc + _nt(hl, jnp.concatenate([high, gap, low, gap], 0))
        return acc

    acc = lax.fori_loop(0, BX * BY, first_gram, jnp.zeros((96, NZ), jnp.float32))

    def edge_x(y, _):
        above(BX, y)
        return 0

    def edge_y(x, _):
        above(x, BY)
        return 0

    lax.fori_loop(0, BY + 1, edge_x, 0)
    lax.fori_loop(0, BX, edge_y, 0)

    def q_at(k, x, y, ct):
        return qm[k, x, y, ct]

    def add_w(k, ex, x, y, ct, value):
        if x == ex and ex > 0:
            wf[k, x, y, ct] += value
        else:
            wf[k, x, y, ct] = value

    _apply(q_at, e_at, add_w, range(BX), 0, BY, True)

    gap8 = jnp.zeros((8, NZ), jnp.float32)
    gap32 = jnp.zeros((32, NZ), jnp.bfloat16)

    def second_gram(t, acc):
        x, y = t // (BY + 1), t % (BY + 1)
        fr = free[x + 1, y + 1]
        mine = jnp.where((x < BX) & (y < BY), 1.0, 0.0).astype(jnp.float32)
        for k in range(3):
            w = fr * wf[k, x, y] + (mine * (1.0 - fr)) * qf[k, x, y]
            high, low = _split(jnp.concatenate([_rows(w), gap8], 0))
            acc = acc + _nt(split[k, x, y], jnp.concatenate([high, gap32, low, gap32], 0))
        return acc

    acc2 = lax.fori_loop(0, (BX + 1) * (BY + 1), second_gram, jnp.zeros((96, NZ), jnp.float32))

    lane = lax.broadcasted_iota(jnp.int32, (CASES, NZ), 1)
    both = acc[:48] + acc[48:]
    both = both + pltpu.roll(both, 64, axis=1)
    last = acc2[24:48] + acc2[72:]
    last = last + pltpu.roll(last, 64, axis=1)
    table = jnp.where(
        lane < 48, both[:24], jnp.where(lane < 96, pltpu.roll(both[24:], 48, axis=1), pltpu.roll(last, 96, axis=1)))

    slot = 0
    for n, phase in enumerate(phases):
        gram_send[n] = table
        group = []
        for m, (ox, oy) in enumerate(phase):
            group.append(pltpu.make_async_remote_copy(
                gram_send.at[n], gram_recv.at[slot + m], g_send.at[slot + m], g_recv.at[slot + m],
                device_id=(i ^ ox, j ^ oy), device_id_type=MESH))
        for copy in group:
            copy.start()
        for copy in group:
            copy.wait()
        terms = [table] + [gram_recv[slot + m] for m in range(len(phase))]
        while len(terms) > 1:
            terms = [terms[t] + terms[t + 1] for t in range(0, len(terms), 2)]
        table = terms[0]
        slot += len(phase)

    mix = _solve(table)
    half = jnp.where(lane < 48, mix, 0.0)
    mix = half + pltpu.roll(half, 48, axis=1)
    mix = jnp.concatenate([mix, gap8], 0)
    high, low = _split(mix)
    coefs = jnp.concatenate([high, low], 0)[:, :96]

    def combine(t, _):
        x, y = t // (BY + 1), t % (BY + 1)
        fr = free[x + 1, y + 1]
        for k in range(3):
            u = jnp.dot(coefs, split[k, x, y], preferred_element_type=jnp.float32)
            u = u[:24] + u[32:56]
            disp[k, x, y] = fr * u.reshape(CT, 8, NZ)
        return 0

    lax.fori_loop(0, (BX + 1) * (BY + 1), combine, 0)

    def s_at(k, x, y, ct):
        return disp[k, x, y, ct]

    for x in range(BX):
        energy[x] = jnp.zeros((BY, 8, NZ), jnp.float32)

    def energies(ct, _):
        for x in range(BX):
            first = _stage(s_at, x, 0, ct)

            def step(y, state, x=x):
                s1 = _stage(s_at, x, y + 1, ct)
                energy[x, y] += _density_of_energy(_modes(dict(zip(KEYS, state)), s1))
                return tuple(s1[key] for key in KEYS)

            lax.fori_loop(0, BY, step, tuple(first[key] for key in KEYS), unroll=2)
        return 0

    lax.fori_loop(0, CT, energies, 0)

    rho = [0.3 + 0.7 * lev[2 + x, 2 : 2 + BY, 0, :].astype(jnp.float32) / (LEVELS - 1) for x in range(BX)]
    for x in range(BX):
        sens = -3.0 * rho[x] * rho[x] * jnp.sum(energy[x], axis=1) / CASES
        vals[2 + x, BY : 2 * BY] = rho[x] * sens
    group = []
    for n, (dx, dy) in enumerate(NEIGHBOURS):
        mine = vals.at[2 : 2 + BX, BY : 2 * BY]
        at_x, at_y = 2 - BX * dx, BY - BY * dy
        group.append(pltpu.make_async_remote_copy(
            mine, vals.at[at_x : at_x + BX, at_y : at_y + BY], v_send.at[n], v_recv.at[n],
            device_id=there(dx, dy), device_id_type=MESH))
    for copy in group:
        copy.start()

    grid_y = j * BY - BY + lax.broadcasted_iota(jnp.int32, (3 * BY, NZ), 0)
    ok_y = (grid_y >= 0) & (grid_y < ny * BY)

    def present(p):
        gx = i * BX + p - 2
        return jnp.where(ok_y & (gx >= 0) & (gx < nx * BX), 1.0, 0.0).astype(jnp.float32)

    def spread(p, v):
        zsum[p, 0] = v
        zsum[p, 1] = _shift(v, 1) + _shift(v, -1)
        zsum[p, 2] = _shift(v, 2) + _shift(v, -2)

    def near(p, dy, dz):
        return zsum[p, dz, BY + dy : 2 * BY + dy]

    for p in range(BX + 4):
        spread(p, present(p))
    weights = _cone(near)
    for copy in group:
        copy.wait()
    for p in range(BX + 4):
        spread(p, jnp.where(present(p) > 0.0, vals[p], 0.0))
    sums = _cone(near)
    for x in range(BX):
        out[x] = sums[x] / (rho[x] * weights[x])


def _phases(nx, ny):
    groups = [[(1, 0)], [(2, 0), (0, 1), (2, 1)]]
    groups.append([(4 * o, 0) for o in range(1, nx // 4)])
    groups.append([(0, 2 * o) for o in range(1, ny // 2)])
    return [g for g in groups if g]


def solution(mesh):
    nx, ny = mesh.shape["gx"], mesh.shape["gy"]
    phases = _phases(nx, ny)
    slots = sum(len(g) for g in phases)
    f32 = jnp.float32
    dma = pltpu.SemaphoreType.DMA
    any_space = pl.BlockSpec(memory_space=pl.ANY)

    def local(forces, levels, supports):
        return pl.pallas_call(
            functools.partial(_kernel, nx, ny, phases),
            out_shape=jax.ShapeDtypeStruct((BX, BY, NZ), f32),
            in_specs=[any_space] * 3,
            out_specs=pl.BlockSpec(memory_space=pltpu.VMEM),
            scratch_shapes=[
                pltpu.VMEM((3 * CASES * BX * BY, NZ), f32),
                pltpu.VMEM((BX + 4, BY + 4, 1, NZ), jnp.int32),
                pltpu.VMEM((BX + 3, BY + 3, 1, NZ), jnp.int32),
                pltpu.VMEM((BX + 4, BY + 4, 8, NZ), f32),
                pltpu.VMEM((BX + 4, BY + 4, 8, NZ), f32),
                pltpu.VMEM((BX + 3, BY + 3, 8, NZ), f32),
                pltpu.VMEM((BX + 3, BY + 3, 8, NZ), f32),
                pltpu.VMEM((3, BX + 3, BY + 3, CT, 8, NZ), f32),
                pltpu.VMEM((3, BX + 3, BY + 3, CT, 8, NZ), f32),
                pltpu.VMEM((3, BX + 3, BY + 3, CT, 8, NZ), f32),
                pltpu.VMEM((3, BX + 1, BY + 2, CT, 8, NZ), f32),
                pltpu.VMEM((3, BX + 1, BY + 1, CT, 8, NZ), f32),
                pltpu.VMEM((3, BX + 1, BY + 1, CT, 8, NZ), f32),
                pltpu.VMEM((3, BX + 1, BY + 1, CT, 8, NZ), f32),
                pltpu.VMEM((3, BX + 1, BY + 1, 96, NZ), jnp.bfloat16),
                pltpu.VMEM((3, BX + 1, BY + 1, CT, 8, NZ), f32),
                pltpu.VMEM((BX, BY, 8, NZ), f32),
                pltpu.VMEM((BX + 4, 3 * BY, NZ), f32),
                pltpu.VMEM((BX + 4, 3, 3 * BY, NZ), f32),
                pltpu.VMEM((len(phases), CASES, NZ), f32),
                pltpu.VMEM((slots, CASES, NZ), f32),
                dma((3,)),
                dma((8,)), dma((8,)), dma((8,)), dma((8,)), dma((8,)), dma((8,)), dma((8,)), dma((8,)),
                dma((slots,)), dma((slots,)),
            ],
            compiler_params=pltpu.CompilerParams(collective_id=0, has_side_effects=True),
        )(
            forces.reshape(3 * CASES * BX * BY, NZ),
            levels.reshape(BX, BY, 1, NZ),
            supports.reshape(BX, BY, 1, NZ),
        )

    return jax.shard_map(
        local,
        mesh=mesh,
        in_specs=(P(None, None, "gx", "gy", None), P("gx", "gy", None), P("gx", "gy", None)),
        out_specs=P("gx", "gy", None),
        check_vma=False,
    )
```

time: 558 us -> 85.8 us (0.15)
  the two profiles are of different devices: /device:TPU:8 before, /device:TPU:1 now
where the time goes in v1:
time: 85.8 us; the launch traced here: 85.6 us
  Pallas kernels  84.3 us (98%)
  local copies, waits for them, and re-layouts  1.3 us (2%)
    pallas_call x1, Pallas kernels, local(): pl.pallas_call(functools.partial(_kernel, nx, ny, phases), out_shape=jax....  84.3 us

profile of v1, /device:TPU:1, one launch (start us, length us, event | category | flops | bytes accessed | tf_op | source)
XLA Modules:
  0.0 85.6 jit_solution(16211158065126875935)
XLA Ops:
  0.0 84.3 %shard_map.37 = f32[2,8,128]{2,1,0:T(8,128)} custom-call(f32[1152,128]{1,0:T(8,128)} %bitcast.3, s32[2,8,1,128]{3,2,1,0:T(1,128)} %bitcast.4, s32[2,8,1,128]{3,2,1,0:T(1,128)} %bitcast.5), custom_call_target="tpu_custom_call" | custom-call | tf_op jit(solution)/shard_map/pallas_call | solution.py:599
  84.3 1.3 %copy.5 = f32[2,8,128]{2,1,0:T(8,128)} copy(f32[2,8,128]{2,1,0:T(8,128)} %shard_map.37) | data formatting | bytes 16384

commit v2 on v1

v2 whole, which is shorter than its diff:
```python
import functools
import math

import jax
import jax.numpy as jnp
import numpy as np
from jax import lax
from jax.experimental import pallas as pl
from jax.experimental.pallas import tpu as pltpu
from jax.sharding import PartitionSpec as P

MESH = pl.DeviceIdType.MESH
CASES = 24
LEVELS = 16
LOAD = 0.2
BX, BY, NZ = 2, 8, 128
CT = 3


def element_matrix():
    poisson = 0.3
    lame_first = poisson / ((1.0 + poisson) * (1.0 - 2.0 * poisson))
    lame_shear = 1.0 / (2.0 * (1.0 + poisson))
    elastic = np.zeros((6, 6))
    elastic[:3, :3] = lame_first
    for position in range(3):
        elastic[position, position] += 2.0 * lame_shear
        elastic[position + 3, position + 3] = lame_shear
    points = [0.5 - 0.5 / math.sqrt(3.0), 0.5 + 0.5 / math.sqrt(3.0)]
    matrix = np.zeros((24, 24))
    for point_x in points:
        for point_y in points:
            for point_z in points:
                coords = (point_x, point_y, point_z)
                strain = np.zeros((6, 24))
                for corner in range(8):
                    bits = (corner >> 2 & 1, corner >> 1 & 1, corner & 1)
                    shape = [coords[n] if bits[n] else 1.0 - coords[n] for n in range(3)]
                    slopes = [1.0 if bits[n] else -1.0 for n in range(3)]
                    slope_x = slopes[0] * shape[1] * shape[2]
                    slope_y = shape[0] * slopes[1] * shape[2]
                    slope_z = shape[0] * shape[1] * slopes[2]
                    o = 3 * corner
                    strain[0, o] = slope_x
                    strain[1, o + 1] = slope_y
                    strain[2, o + 2] = slope_z
                    strain[3, o] = slope_y
                    strain[3, o + 1] = slope_x
                    strain[4, o + 1] = slope_z
                    strain[4, o + 2] = slope_y
                    strain[5, o] = slope_z
                    strain[5, o + 2] = slope_x
                matrix = matrix + strain.T @ elastic @ strain / 8.0
    return matrix


KE = element_matrix()
DIAG = float(KE[0, 0])


def parity_matrix():
    walsh = np.ones((8, 8))
    for mode in range(8):
        for corner in range(8):
            for n in range(3):
                if mode >> n & 1:
                    walsh[mode, corner] *= 2 * (corner >> n & 1) - 1
    big = np.kron(walsh, np.eye(3))
    return big @ KE @ big.T / 64.0


KP = parity_matrix()
UNIT = ((1, 0, 0), (0, 1, 0), (0, 0, 1))


def _flip(p, k):
    return tuple(a ^ b for a, b in zip(p, UNIT[k]))


def _kp(m, n):
    at = [3 * (4 * p[0] + 2 * p[1] + p[2]) + k for k, p in (m, n)]
    return float(KP[at[0], at[1]])


NORMAL = [(k, UNIT[k]) for k in range(3)]
BEND = [(k, _flip((1, 1, 1), k)) for k in range(3)]
PAIRS = [[(k, _flip(UNIT[s], k)) for k in range(3) if k != s] for s in range(3)]
SHEAR = []
TWIST = []
for _s in range(3):
    _a, _b = [k for k in range(3) if k != _s]
    SHEAR.append([(_a, UNIT[_b]), (_b, UNIT[_a])])
    TWIST.append((_s, (1, 1, 1)))
N_OFF = _kp(NORMAL[0], NORMAL[1])
N_DIA = _kp(NORMAL[0], NORMAL[0]) - N_OFF
P_OFF = _kp(PAIRS[0][0], PAIRS[0][1])
P_DIA = _kp(PAIRS[0][0], PAIRS[0][0]) - P_OFF
S_ALL = _kp(SHEAR[0][0], SHEAR[0][0])
T_ALL = _kp(TWIST[0], TWIST[0])
B_OFF = _kp(BEND[0], BEND[1])
B_DIA = _kp(BEND[0], BEND[0]) - B_OFF


def _span(d, low, high, size):
    a = max(0, low + d * size)
    b = min(size, high + 1 + d * size)
    return a, a - d * size, b - a


NEIGHBOURS = [(dx, dy) for dx in (-1, 0, 1) for dy in (-1, 0, 1) if dx or dy]


def _shift(x, by):
    lane = lax.broadcasted_iota(jnp.int32, x.shape, x.ndim - 1)
    r = pltpu.roll(x, (-by) % NZ, axis=x.ndim - 1)
    ok = lane < NZ - by if by > 0 else lane >= -by
    return jnp.where(ok, r, 0.0)


def _stage(u_at, ex, y, ct):
    out = {}
    for k in range(3):
        for pz in (0, 1):
            u0, u1 = u_at(k, pz, ex, y, ct), u_at(k, pz, ex + 1, y, ct)
            out[k, 0, pz] = u0 + u1
            out[k, 1, pz] = u1 - u0
    return out


KEYS = [(k, px, pz) for k in range(3) for px in (0, 1) for pz in (0, 1)]


def _modes(s0, s1):
    out = {}
    for k, px, pz in KEYS:
        if (px, pz) != (0, 0):
            out[k, (px, 0, pz)] = s0[k, px, pz] + s1[k, px, pz]
        out[k, (px, 1, pz)] = s1[k, px, pz] - s0[k, px, pz]
    return out


SCALES = sorted({np.float32(c) for c in (N_OFF, N_DIA, P_OFF, P_DIA, S_ALL, T_ALL, B_OFF, B_DIA)})


def _stress(u, e_at):
    def e(c):
        return e_at(SCALES.index(np.float32(c)))

    g = {}
    for group, off, dia in ((NORMAL, N_OFF, N_DIA), (BEND, B_OFF, B_DIA)):
        total = (u[group[0]] + u[group[1]] + u[group[2]]) * e(off)
        for m in group:
            g[m] = u[m] * e(dia) + total
    for a, b in PAIRS:
        total = (u[a] + u[b]) * e(P_OFF)
        g[a] = u[a] * e(P_DIA) + total
        g[b] = u[b] * e(P_DIA) + total
    for a, b in SHEAR:
        g[a] = g[b] = (u[a] + u[b]) * e(S_ALL)
    for m in TWIST:
        g[m] = u[m] * e(T_ALL)
    return g


def _density_of_energy(u):
    def sq(x):
        return x * x

    e = N_OFF * sq(u[NORMAL[0]] + u[NORMAL[1]] + u[NORMAL[2]])
    e = e + N_DIA * (sq(u[NORMAL[0]]) + sq(u[NORMAL[1]]) + sq(u[NORMAL[2]]))
    e = e + B_OFF * sq(u[BEND[0]] + u[BEND[1]] + u[BEND[2]])
    e = e + B_DIA * (sq(u[BEND[0]]) + sq(u[BEND[1]]) + sq(u[BEND[2]]))
    off = dia = she = twi = 0.0
    for a, b in PAIRS:
        off = off + sq(u[a] + u[b])
        dia = dia + sq(u[a]) + sq(u[b])
    for a, b in SHEAR:
        she = she + sq(u[a] + u[b])
    for m in TWIST:
        twi = twi + sq(u[m])
    return e + P_OFF * off + P_DIA * dia + S_ALL * she + T_ALL * twi


def _apply(u_at, e_at, add, layers, y_low, columns, close, unroll=2):
    def tile(ct, _):
        for ex in layers:
            first = _stage(u_at, ex, y_low, ct)
            zero = jnp.zeros((8, NZ), jnp.float32)

            def emit(y, h, ex=ex):
                for k in range(3):
                    for pz in (0, 1):
                        p0, p1 = h[k, 0, pz], h[k, 1, pz]
                        add(k, pz, ex, ex, y, ct, p0, p1)
                        add(k, pz, ex, ex + 1, y, ct, p0, p1)

            def step(t, state, ex=ex):
                s0 = dict(zip(KEYS, state[0]))
                carry = dict(zip(KEYS, state[1]))
                y = y_low + t
                s1 = _stage(u_at, ex, y + 1, ct)
                g = _stress(_modes(s0, s1), functools.partial(e_at, ex, y))
                h, later = {}, {}
                for key in KEYS:
                    k, px, pz = key
                    g1 = g[k, (px, 1, pz)]
                    g0 = g.get((k, (px, 0, pz)))
                    if g0 is None:
                        h[key] = carry[key] - g1
                        later[key] = g1
                    else:
                        h[key] = carry[key] + (g0 - g1)
                        later[key] = g0 + g1
                emit(y, h)
                return tuple(s1[key] for key in KEYS), tuple(later[key] for key in KEYS)

            state = (tuple(first[key] for key in KEYS), (zero,) * len(KEYS))
            if columns == 1:
                state = step(0, state)
            else:
                state = lax.fori_loop(0, columns, step, state, unroll=unroll)
            if close:
                emit(y_low + columns, dict(zip(KEYS, state[1])))
        return 0

    lax.fori_loop(0, CT, tile, 0)


def _sum_diff(u):
    up = _shift(u, 1)
    return u + up, up - u


def _gather_z(s, d):
    return (s - d) + _shift(s + d, -1)


def _loop2(xs, ys, body, state=0, unroll=1):
    def outer(x, state):
        return lax.fori_loop(ys[0], ys[1], lambda y, st: body(x, y, st), state, unroll=unroll)

    return lax.fori_loop(xs[0], xs[1], outer, state)


def _split(x):
    scaled = x * 65537.0
    high = scaled - (scaled - x)
    return high.astype(jnp.bfloat16), (x - high).astype(jnp.bfloat16)


def _rows(x):
    return x.reshape(CASES, NZ)


def _nt(a, b):
    return lax.dot_general(a, b, (((1,), (1,)), ((), ())), preferred_element_type=jnp.float32)


def _system(table):
    lane = lax.broadcasted_iota(jnp.int32, (CASES, NZ), 1)

    def left(x, by):
        return pltpu.roll(x, (-by) % NZ, axis=1)

    def join(a, b):
        return jnp.where(lane < 24, a, jnp.where(lane < 48, b, 0.0))

    blocks = [
        join(table, left(table, 24)),
        join(left(table, 48), jnp.zeros_like(table)),
        join(left(table, 24), left(table, 48)),
    ]
    return [b[8 * i : 8 * i + 8] for b in blocks for i in range(3)]


def _eliminate(tiles, scales, steps):
    lane = lax.broadcasted_iota(jnp.int32, (1, NZ), 1)
    for j in steps:
        row = tiles[j // 8][j % 8 : j % 8 + 1]
        scale = 1.0 / row[:, j : j + 1]
        factor = jnp.where(lane == j, 0.0, row * scale)
        scales = jnp.where(lane == j, scale, scales)
        for t in range((j + 1) // 8, 9):
            tiles[t] = tiles[t] - tiles[t][:, j : j + 1] * factor
    return tiles, scales


WEIGHT = {}
for _dx in range(-2, 3):
    for _dy in range(-2, 3):
        for _dz in range(3):
            _w = 2.5 - math.sqrt(_dx * _dx + _dy * _dy + _dz * _dz)
            if _w > 0.0:
                WEIGHT[_dx, _dy, _dz] = _w


def _cone(planes):
    result = []
    for xo in range(BX):
        total = jnp.zeros((BY, NZ), jnp.float32)
        for (dx, dy, dz), w in WEIGHT.items():
            total = total + w * planes(xo + 2 + dx, dy, dz)
        result.append(total)
    return result


SET_A = [(dx, dy, _span(dx, -1, 2, BX), _span(dy, -1, 8, BY)) for dx, dy in NEIGHBOURS]
SET_B = [
    (-1, 0, (1, 3, 1), (0, 0, BY)),
    (0, -1, (0, 0, BX), (1, 9, 1)),
    (-1, 1, (1, 3, 1), (7, -1, 1)),
    (-1, -1, (1, 3, 1), (0, 8, 2)),
    (-1, -1, (0, 2, 1), (1, 9, 1)),
    (1, -1, (1, -1, 1), (1, 9, 1)),
]


def _kernel(nx, ny, phases, forces, levels, supports, out, nat, lev, sup, stiff, stiffz, inv, free, field, dire, masked,
            image, qf, qm, wf, split, disp, energy, vals, zsum, gram_send, gram_recv, local_sem, l_send, l_recv, s_send,
            s_recv, f_send, f_recv, v_send, v_recv, g_send, g_recv):
    i, j = lax.axis_index("gx"), lax.axis_index("gy")

    def there(dx, dy):
        return lax.rem(i + dx + nx, nx), lax.rem(j + dy + ny, ny)

    peers = [there(dx, dy) for dx, dy in NEIGHBOURS]
    for phase in phases:
        for ox, oy in phase:
            peers.append((i ^ ox, j ^ oy))

    c_nat = pltpu.make_async_copy(forces, nat, local_sem.at[0])
    c_lev = pltpu.make_async_copy(levels, lev.at[2 : 2 + BX, 2 : 2 + BY], local_sem.at[1])
    c_sup = pltpu.make_async_copy(supports, sup.at[1 : 1 + BX, 1 : 1 + BY], local_sem.at[2])
    c_nat.start()
    c_lev.start()
    c_sup.start()

    barrier = pltpu.get_barrier_semaphore()
    for peer in peers:
        pl.semaphore_signal(barrier, inc=1, device_id=peer, device_id_type=MESH)

    c_nat.wait()

    def arrange(k, _):
        for x in range(BX):
            for y in range(BY):
                rows = nat[pl.ds(k * (CASES * BX * BY) + x * BY + y, CASES, stride=BX * BY), :]
                field[k, 1 + x, 1 + y] = rows.reshape(CT, 8, NZ)
        return 0

    lax.fori_loop(0, 3, arrange, 0)
    c_lev.wait()
    c_sup.wait()

    pl.semaphore_wait(barrier, len(peers))

    small, set_a, set_b = [], [], []
    for n, (dx, dy) in enumerate(NEIGHBOURS):
        (a, b, c), (d, e, f) = _span(dx, -2, 3, BX), _span(dy, -2, 9, BY)
        small.append(pltpu.make_async_remote_copy(
            levels.at[a : a + c, d : d + f], lev.at[b + 2 : b + 2 + c, e + 2 : e + 2 + f],
            l_send.at[n], l_recv.at[n], device_id=there(dx, dy), device_id_type=MESH))
        (a, b, c), (d, e, f) = _span(dx, -1, 3, BX), _span(dy, -1, 9, BY)
        small.append(pltpu.make_async_remote_copy(
            supports.at[a : a + c, d : d + f], sup.at[b + 1 : b + 1 + c, e + 1 : e + 1 + f],
            s_send.at[n], s_recv.at[n], device_id=there(dx, dy), device_id_type=MESH))
    for n, (dx, dy, (a, b, c), (d, e, f)) in enumerate(SET_A + SET_B):
        (set_a if n < len(SET_A) else set_b).append(pltpu.make_async_remote_copy(
            field.at[:, a + 1 : a + 1 + c, d + 1 : d + 1 + f], field.at[:, b + 1 : b + 1 + c, e + 1 : e + 1 + f],
            f_send.at[n], f_recv.at[n], device_id=there(dx, dy), device_id_type=MESH))
    for copy in small + set_a + set_b:
        copy.start()
    for copy in small:
        copy.wait_recv()

    def inside(x, y):
        gx, gy = i * BX + x, j * BY + y
        ok = (gx >= 0) & (gx < nx * BX) & (gy >= 0) & (gy < ny * BY)
        return jnp.where(ok, 1.0, 0.0).astype(jnp.float32)

    def moduli(x, y, _):
        level = jnp.broadcast_to(lev[x, y], (8, NZ)).astype(jnp.float32)
        rho = 0.3 + 0.7 * level / (LEVELS - 1)
        e = rho * rho * rho * inside(x - 2, y - 2)
        for n, c in enumerate(SCALES):
            stiff[x, y, n] = e * float(c)
        stiffz[x, y] = (e + _shift(e, -1)) * DIAG
        return 0

    _loop2((0, BX + 4), (0, BY + 4), moduli, unroll=4)

    def nodal(x, y, _):
        fr = (1 - jnp.broadcast_to(sup[x, y], (8, NZ))).astype(jnp.float32) * inside(x - 1, y - 1)
        total = (stiffz[x, y] + stiffz[x + 1, y]) + (stiffz[x, y + 1] + stiffz[x + 1, y + 1])
        free[x, y] = fr
        inv[x, y] = 1.0 / (fr * total + (1.0 - fr))
        return 0

    _loop2((0, BX + 3), (0, BY + 3), nodal, unroll=3)

    def search(x, y, _):
        fr, iv = free[x, y], inv[x, y]
        for k in range(3):
            d = iv * (LOAD * fr * field[k, x, y])
            dire[k, x, y] = d
            s, t = _sum_diff(fr * d)
            masked[k, 0, x, y] = s
            masked[k, 1, x, y] = t
        return 0

    _loop2((1, 1 + BX), (1, 1 + BY), search, unroll=2)
    for copy in set_a:
        copy.wait_recv()
    _loop2((0, 1), (0, BY + 2), search, unroll=2)
    _loop2((BX + 1, BX + 2), (0, BY + 2), search, unroll=2)
    for y in (0, BY + 1):
        _loop2((1, 1 + BX), (y, y + 1), search)

    def u_at(k, pz, x, y, ct):
        return masked[k, pz, x + 1, y + 1, ct]

    def e_at(x, y, n):
        return stiff[x + 2, y + 2, n]

    def adder(ref, fresh, shift, planes):
        def add(k, pz, ex, x, y, ct, p0, p1):
            if x not in planes:
                return
            value = p0 - p1 if x == ex else p0 + p1
            if fresh(ex, x):
                ref[k, pz, x, y + shift, ct] = value
            else:
                ref[k, pz, x, y + shift, ct] += value
        return add

    at_nodes = range(BX + 1)
    _apply(u_at, e_at, adder(image, lambda ex, x: x == ex + 1, 1, at_nodes), range(-1, BX), -1, BY + 1, True, unroll=3)

    gap = jnp.zeros((16, NZ), jnp.bfloat16)
    gap8 = jnp.zeros((8, NZ), jnp.float32)
    gap32 = jnp.zeros((32, NZ), jnp.bfloat16)

    def above(x, y):
        fr, iv = free[x + 1, y + 1], inv[x + 1, y + 1]
        rows, images = [], []
        for k in range(3):
            d = dire[k, x + 1, y + 1]
            im = fr * _gather_z(image[k, 0, x, y + 1], image[k, 1, x, y + 1]) + (1.0 - fr) * d
            q = iv * im
            qf[k, x, y] = q
            s, t = _sum_diff(fr * q)
            qm[k, 0, x, y] = s
            qm[k, 1, x, y] = t
            high, low = _split(jnp.concatenate([_rows(d), _rows(q)], 0))
            hl = jnp.concatenate([high, low], 0)
            split[k, x, y] = hl
            rows.append(hl)
            images.append(im)
        return rows, images, fr

    def first_gram(x, y, acc):
        rows, images, fr = above(x, y)
        right = []
        for k in range(3):
            r0 = LOAD * fr * field[k, x + 1, y + 1]
            high, low = _split(jnp.concatenate([_rows(images[k]), _rows(r0)], 0))
            right.append(jnp.concatenate([high, gap, low, gap], 0))
        return acc + _nt(jnp.concatenate(rows, 1), jnp.concatenate(right, 1))

    acc = _loop2((0, BX), (0, BY), first_gram, jnp.zeros((96, NZ), jnp.float32))
    lane = lax.broadcasted_iota(jnp.int32, (CASES, NZ), 1)
    both = acc[:48] + acc[48:]
    both = both + pltpu.roll(both, 64, axis=1)
    table = jnp.where(lane < 48, both[:24], jnp.where(lane < 96, pltpu.roll(both[24:], 48, axis=1), 0.0))

    per_round = sum(len(p) for p in phases)

    def begin(turn, n, value):
        slot = turn * per_round + sum(len(p) for p in phases[:n])
        gram_send[turn * len(phases) + n] = value
        group = [pltpu.make_async_remote_copy(
            gram_send.at[turn * len(phases) + n], gram_recv.at[slot + m], g_send.at[slot + m], g_recv.at[slot + m],
            device_id=(i ^ ox, j ^ oy), device_id_type=MESH) for m, (ox, oy) in enumerate(phases[n])]
        for copy in group:
            copy.start()
        sent.extend(group)
        return value, slot, group

    def finish(going):
        value, slot, group = going
        for copy in group:
            copy.wait_recv()
        terms = [value] + [gram_recv[slot + m] for m in range(len(group))]
        while len(terms) > 1:
            terms = [terms[t] + terms[t + 1] for t in range(0, len(terms), 2)]
        return terms[0]

    sent = []
    todo = list(range(len(phases)))
    going = begin(0, todo.pop(0), table)

    for copy in set_b:
        copy.wait_recv()
    _loop2((BX + 2, BX + 3), (0, BY + 3), search, unroll=2)
    _loop2((0, BX + 2), (BY + 2, BY + 3), search, unroll=2)
    _apply(u_at, e_at, adder(image, lambda ex, x: False, 1, at_nodes), range(-1, BX), BY, 1, False)
    if todo:
        going = begin(0, todo.pop(0), finish(going))
    _apply(u_at, e_at, adder(image, lambda ex, x: False, 1, at_nodes), range(BX, BX + 1), -1, BY + 2, False, unroll=2)

    def edge(x, y, _):
        above(x, y)
        return 0

    _loop2((BX, BX + 1), (0, BY + 1), edge, unroll=3)
    _loop2((0, BX), (BY, BY + 1), edge)
    if todo:
        going = begin(0, todo.pop(0), finish(going))

    def q_at(k, pz, x, y, ct):
        return qm[k, pz, x, y, ct]

    _apply(q_at, e_at, adder(wf, lambda ex, x: x == ex + 1 or ex == 0, 0, at_nodes), range(BX), 0, BY, True, unroll=2)
    if todo:
        going = begin(0, todo.pop(0), finish(going))

    def second_gram(x, y, acc):
        fr = free[x + 1, y + 1]
        mine = jnp.where((x < BX) & (y < BY), 1.0, 0.0).astype(jnp.float32)
        right = []
        for k in range(3):
            w = fr * _gather_z(wf[k, 0, x, y], wf[k, 1, x, y]) + (mine * (1.0 - fr)) * qf[k, x, y]
            high, low = _split(jnp.concatenate([_rows(w), gap8], 0))
            right.append(jnp.concatenate([high, gap32, low, gap32], 0))
        left = jnp.concatenate([split[k, x, y] for k in range(3)], 1)
        return acc + _nt(left, jnp.concatenate(right, 1))

    acc2 = _loop2((0, BX + 1), (0, BY + 1), second_gram, jnp.zeros((96, NZ), jnp.float32), unroll=3)
    last = acc2[24:48] + acc2[72:]
    last = last + pltpu.roll(last, 64, axis=1)
    n_going = begin(1, 0, last)
    table = finish(going)
    todo = list(range(1, len(phases)))
    if todo:
        n_going = begin(1, todo.pop(0), finish(n_going))
    tiles, scales = _eliminate(_system(table), jnp.zeros((1, NZ), jnp.float32), range(24))
    if todo:
        n_going = begin(1, todo.pop(0), finish(n_going))

    grid_y = j * BY - BY + lax.broadcasted_iota(jnp.int32, (3 * BY, NZ), 0)
    ok_y = (grid_y >= 0) & (grid_y < ny * BY)

    def present(p):
        gx = i * BX + p - 2
        return jnp.where(ok_y & (gx >= 0) & (gx < nx * BX), 1.0, 0.0).astype(jnp.float32)

    def spread(p, v):
        zsum[p, 0] = v
        zsum[p, 1] = _shift(v, 1) + _shift(v, -1)
        zsum[p, 2] = _shift(v, 2) + _shift(v, -2)

    def near(p, dy, dz):
        return zsum[p, dz, BY + dy : 2 * BY + dy]

    for p in range(BX + 4):
        spread(p, present(p))
    weights = _cone(near)
    rho = [0.3 + 0.7 * lev[2 + x, 2 : 2 + BY, 0, :].astype(jnp.float32) / (LEVELS - 1) for x in range(BX)]

    if todo:
        n_going = begin(1, todo.pop(0), finish(n_going))
    last = finish(n_going)
    last = jnp.where(lane < 24, last, 0.0)
    last = pltpu.roll(last, 24, axis=1)
    for t in range(3):
        tiles[3 + t] = tiles[3 + t] + last[8 * t : 8 * t + 8]
    tiles, scales = _eliminate(tiles, scales, range(24, 48))
    half = jnp.concatenate(tiles[6:], 0) * scales
    mix = half + pltpu.roll(half, 48, axis=1)
    mix = jnp.concatenate([mix, gap8], 0)
    high, low = _split(mix)
    coefs = jnp.concatenate([high, low], 0)[:, :96]

    def combine(x, y, _):
        fr = free[x + 1, y + 1]
        for k in range(3):
            u = jnp.dot(coefs, split[k, x, y], preferred_element_type=jnp.float32)
            u = u[:24] + u[32:56]
            s, t = _sum_diff(fr * u.reshape(CT, 8, NZ))
            disp[k, 0, x, y] = s
            disp[k, 1, x, y] = t
        return 0

    _loop2((0, BX + 1), (0, BY + 1), combine, unroll=3)

    def s_at(k, pz, x, y, ct):
        return disp[k, pz, x, y, ct]

    for x in range(BX):
        energy[x] = jnp.zeros((BY, 8, NZ), jnp.float32)

    def energies(ct, _):
        for x in range(BX):
            first = _stage(s_at, x, 0, ct)

            def step(y, state, x=x):
                s1 = _stage(s_at, x, y + 1, ct)
                energy[x, y] += _density_of_energy(_modes(dict(zip(KEYS, state)), s1))
                return tuple(s1[key] for key in KEYS)

            lax.fori_loop(0, BY, step, tuple(first[key] for key in KEYS), unroll=2)
        return 0

    lax.fori_loop(0, CT, energies, 0)

    for x in range(BX):
        sens = -3.0 * rho[x] * rho[x] * jnp.sum(energy[x], axis=1) / CASES
        vals[2 + x, BY : 2 * BY] = rho[x] * sens
    group = []
    for n, (dx, dy) in enumerate(NEIGHBOURS):
        at_x, at_y = 2 - BX * dx, BY - BY * dy
        group.append(pltpu.make_async_remote_copy(
            vals.at[2 : 2 + BX, BY : 2 * BY], vals.at[at_x : at_x + BX, at_y : at_y + BY], v_send.at[n], v_recv.at[n],
            device_id=there(dx, dy), device_id_type=MESH))
    for copy in group:
        copy.start()
    for copy in small + set_a + set_b + sent:
        copy.wait_send()
    for copy in group:
        copy.wait_recv()
    for p in range(BX + 4):
        spread(p, jnp.where(present(p) > 0.0, vals[p], 0.0))
    sums = _cone(near)
    for x in range(BX):
        out[x] = sums[x] / (rho[x] * weights[x])
    for copy in group:
        copy.wait_send()


def _phases(nx, ny):
    groups = [[(1, 0)], [(2, 0), (0, 1), (2, 1)]]
    groups.append([(4 * o, 0) for o in range(1, nx // 4)])
    groups.append([(0, 2 * o) for o in range(1, ny // 2)])
    return [g for g in groups if g]


def solution(mesh):
    nx, ny = mesh.shape["gx"], mesh.shape["gy"]
    phases = _phases(nx, ny)
    slots = sum(len(g) for g in phases)
    f32 = jnp.float32
    dma = pltpu.SemaphoreType.DMA
    any_space = pl.BlockSpec(memory_space=pl.ANY)

    def local(forces, levels, supports):
        return pl.pallas_call(
            functools.partial(_kernel, nx, ny, phases),
            out_shape=jax.ShapeDtypeStruct((BX, BY, NZ), f32),
            in_specs=[any_space] * 3,
            out_specs=pl.BlockSpec(memory_space=pltpu.VMEM),
            scratch_shapes=[
                pltpu.VMEM((3 * CASES * BX * BY, NZ), f32),
                pltpu.VMEM((BX + 4, BY + 4, 1, NZ), jnp.int32),
                pltpu.VMEM((BX + 3, BY + 3, 1, NZ), jnp.int32),
                pltpu.VMEM((BX + 4, BY + 4, len(SCALES), 8, NZ), f32),
                pltpu.VMEM((BX + 4, BY + 4, 8, NZ), f32),
                pltpu.VMEM((BX + 3, BY + 3, 8, NZ), f32),
                pltpu.VMEM((BX + 3, BY + 3, 8, NZ), f32),
                pltpu.VMEM((3, BX + 3, BY + 3, CT, 8, NZ), f32),
                pltpu.VMEM((3, BX + 3, BY + 3, CT, 8, NZ), f32),
                pltpu.VMEM((3, 2, BX + 3, BY + 3, CT, 8, NZ), f32),
                pltpu.VMEM((3, 2, BX + 1, BY + 2, CT, 8, NZ), f32),
                pltpu.VMEM((3, BX + 1, BY + 1, CT, 8, NZ), f32),
                pltpu.VMEM((3, 2, BX + 1, BY + 1, CT, 8, NZ), f32),
                pltpu.VMEM((3, 2, BX + 1, BY + 1, CT, 8, NZ), f32),
                pltpu.VMEM((3, BX + 1, BY + 1, 96, NZ), jnp.bfloat16),
                pltpu.VMEM((3, 2, BX + 1, BY + 1, CT, 8, NZ), f32),
                pltpu.VMEM((BX, BY, 8, NZ), f32),
                pltpu.VMEM((BX + 4, 3 * BY, NZ), f32),
                pltpu.VMEM((BX + 4, 3, 3 * BY, NZ), f32),
                pltpu.VMEM((2 * len(phases), CASES, NZ), f32),
                pltpu.VMEM((2 * slots, CASES, NZ), f32),
                dma((3,)),
                dma((8,)), dma((8,)), dma((8,)), dma((8,)), dma((14,)), dma((14,)), dma((8,)), dma((8,)),
                dma((2 * slots,)), dma((2 * slots,)),
            ],
            compiler_params=pltpu.CompilerParams(collective_id=0, has_side_effects=True),
        )(
            forces.reshape(3 * CASES * BX * BY, NZ),
            levels.reshape(BX, BY, 1, NZ),
            supports.reshape(BX, BY, 1, NZ),
        )

    return jax.shard_map(
        local,
        mesh=mesh,
        in_specs=(P(None, None, "gx", "gy", None), P("gx", "gy", None), P("gx", "gy", None)),
        out_specs=P("gx", "gy", None),
        check_vma=False,
    )
```

time: 85.8 us -> 68 us (0.79)
  Pallas kernels: 84.3 us -> 66.5 us
    pallas_call x1, Pallas kernels: 84.3 us -> 66.5 us  [local(): pl.pallas_call(functools.partial(_kernel, nx, ny, phases), out_shape=jax....]
where the time goes in v2:
time: 68 us; the launch traced here: 67.8 us
  Pallas kernels  66.5 us (98%)
  local copies, waits for them, and re-layouts  1.3 us (2%)
    pallas_call x1, Pallas kernels, local(): pl.pallas_call(functools.partial(_kernel, nx, ny, phases), out_shape=jax....  66.5 us

profile of v2, /device:TPU:1, one launch (start us, length us, event | category | flops | bytes accessed | tf_op | source)
XLA Modules:
  0.0 67.8 jit_solution(4759938191728164638)
XLA Ops:
  0.0 66.5 %shard_map.37 = f32[2,8,128]{2,1,0:T(8,128)} custom-call(f32[1152,128]{1,0:T(8,128)} %bitcast.3, s32[2,8,1,128]{3,2,1,0:T(1,128)} %bitcast.4, s32[2,8,1,128]{3,2,1,0:T(1,128)} %bitcast.5), custom_call_target="tpu_custom_call" | custom-call | tf_op jit(solution)/shard_map/pallas_call | solution.py:656
  66.5 1.3 %copy.5 = f32[2,8,128]{2,1,0:T(8,128)} copy(f32[2,8,128]{2,1,0:T(8,128)} %shard_map.37) | data formatting | bytes 16384

commit v3 on v2

--- a/solution.py
+++ b/solution.py
@@ -285,21 +285,27 @@
     return tiles, scales
 
 
-WEIGHT = {}
-for _dx in range(-2, 3):
-    for _dy in range(-2, 3):
-        for _dz in range(3):
-            _w = 2.5 - math.sqrt(_dx * _dx + _dy * _dy + _dz * _dz)
-            if _w > 0.0:
-                WEIGHT[_dx, _dy, _dz] = _w
+def _weight(dx, dy, dz):
+    return max(0.0, 2.5 - math.sqrt(dx * dx + dy * dy + dz * dz))
 
 
 def _cone(planes):
+    by_row = {}
+    for p in range(BX + 4):
+        by_row[p, 0] = planes[p, BY : 2 * BY]
+        for dy in (1, 2):
+            by_row[p, dy] = planes[p, BY + dy : 2 * BY + dy] + planes[p, BY - dy : 2 * BY - dy]
     result = []
     for xo in range(BX):
-        total = jnp.zeros((BY, NZ), jnp.float32)
-        for (dx, dy, dz), w in WEIGHT.items():
-            total = total + w * planes(xo + 2 + dx, dy, dz)
+        total = None
+        for dz in range(3):
+            part = jnp.zeros((BY, NZ), jnp.float32)
+            for dx in range(-2, 3):
+                for dy in range(3):
+                    w = _weight(dx, dy, dz)
+                    if w > 0.0:
+                        part = part + w * by_row[xo + 2 + dx, dy]
+            total = part if dz == 0 else total + (_shift(part, dz) + _shift(part, -dz))
         result.append(total)
     return result
 
@@ -315,9 +321,9 @@
 ]
 
 
-def _kernel(nx, ny, phases, forces, levels, supports, out, nat, lev, sup, stiff, stiffz, inv, free, field, dire, masked,
-            image, qf, qm, wf, split, disp, energy, vals, zsum, gram_send, gram_recv, local_sem, l_send, l_recv, s_send,
-            s_recv, f_send, f_recv, v_send, v_recv, g_send, g_recv):
+def _kernel(nx, ny, phases, phases2, forces, levels, supports, out, nat, lev, sup, stiff, stiffz, inv, free, field, dire, masked,
+            image, qf, qm, wf, split, disp, energy, vals, rim, gram_send, gram_recv, last_send, last_recv, local_sem, l_send, l_recv, s_send,
+            s_recv, f_send, f_recv, v_send, v_recv, g_send, g_recv, n_send, n_recv):
     i, j = lax.axis_index("gx"), lax.axis_index("gy")
 
     def there(dx, dy):
@@ -442,30 +448,27 @@
 
     def above(x, y):
         fr, iv = free[x + 1, y + 1], inv[x + 1, y + 1]
-        rows, images = [], []
+        nodes = []
         for k in range(3):
             d = dire[k, x + 1, y + 1]
             im = fr * _gather_z(image[k, 0, x, y + 1], image[k, 1, x, y + 1]) + (1.0 - fr) * d
             q = iv * im
-            qf[k, x, y] = q
             s, t = _sum_diff(fr * q)
             qm[k, 0, x, y] = s
             qm[k, 1, x, y] = t
-            high, low = _split(jnp.concatenate([_rows(d), _rows(q)], 0))
-            hl = jnp.concatenate([high, low], 0)
-            split[k, x, y] = hl
-            rows.append(hl)
-            images.append(im)
-        return rows, images, fr
+            nodes.append((d, im, q))
+        return nodes, fr
 
     def first_gram(x, y, acc):
-        rows, images, fr = above(x, y)
-        right = []
-        for k in range(3):
+        nodes, fr = above(x, y)
+        left, right = [], []
+        for k, (d, im, q) in enumerate(nodes):
+            qf[k, x, y] = q
             r0 = LOAD * fr * field[k, x + 1, y + 1]
-            high, low = _split(jnp.concatenate([_rows(images[k]), _rows(r0)], 0))
+            left.append(jnp.concatenate(_split(jnp.concatenate([_rows(d), _rows(q)], 0)), 0))
+            high, low = _split(jnp.concatenate([_rows(im), _rows(r0)], 0))
             right.append(jnp.concatenate([high, gap, low, gap], 0))
-        return acc + _nt(jnp.concatenate(rows, 1), jnp.concatenate(right, 1))
+        return acc + _nt(jnp.concatenate(left, 1), jnp.concatenate(right, 1))
 
     acc = _loop2((0, BX), (0, BY), first_gram, jnp.zeros((96, NZ), jnp.float32))
     lane = lax.broadcasted_iota(jnp.int32, (CASES, NZ), 1)
@@ -473,39 +476,57 @@
     both = both + pltpu.roll(both, 64, axis=1)
     table = jnp.where(lane < 48, both[:24], jnp.where(lane < 96, pltpu.roll(both[24:], 48, axis=1), 0.0))
 
-    per_round = sum(len(p) for p in phases)
-
-    def begin(turn, n, value):
-        slot = turn * per_round + sum(len(p) for p in phases[:n])
-        gram_send[turn * len(phases) + n] = value
+    sent = []
+
+    def begin(n, value, groups, source, target, send_sem, recv_sem):
+        slot = sum(len(p) for p in groups[:n])
+        source[n] = value
         group = [pltpu.make_async_remote_copy(
-            gram_send.at[turn * len(phases) + n], gram_recv.at[slot + m], g_send.at[slot + m], g_recv.at[slot + m],
-            device_id=(i ^ ox, j ^ oy), device_id_type=MESH) for m, (ox, oy) in enumerate(phases[n])]
+            source.at[n], target.at[slot + m], send_sem.at[slot + m], recv_sem.at[slot + m],
+            device_id=(i ^ ox, j ^ oy), device_id_type=MESH) for m, (ox, oy) in enumerate(groups[n])]
         for copy in group:
             copy.start()
         sent.extend(group)
-        return value, slot, group
+        return value, slot, group, target
+
+    def begin1(n, value):
+        return begin(n, value, phases, gram_send, gram_recv, g_send, g_recv)
+
+    def begin2(n, value):
+        return begin(n, value, phases2, last_send, last_recv, n_send, n_recv)
 
     def finish(going):
-        value, slot, group = going
+        value, slot, group, target = going
         for copy in group:
             copy.wait_recv()
-        terms = [value] + [gram_recv[slot + m] for m in range(len(group))]
+        terms = [value] + [target[slot + m] for m in range(len(group))]
         while len(terms) > 1:
             terms = [terms[t] + terms[t + 1] for t in range(0, len(terms), 2)]
         return terms[0]
 
-    sent = []
     todo = list(range(len(phases)))
-    going = begin(0, todo.pop(0), table)
+    going = begin1(todo.pop(0), table)
+
+    def pair(left, right, acc):
+        a, b = [], []
+        for u, v in zip(left, right):
+            a.append(jnp.concatenate(_split(jnp.concatenate([_rows(u), gap8], 0)), 0))
+            high, low = _split(jnp.concatenate([_rows(v), gap8], 0))
+            b.append(jnp.concatenate([high, gap32, low, gap32], 0))
+        return acc + _nt(jnp.concatenate(a, 1), jnp.concatenate(b, 1))
+
+    def clamped(x, y, acc):
+        fr = free[x + 1, y + 1]
+        q = [qf[k, x, y] for k in range(3)]
+        return pair(q, [(1.0 - fr) * v for v in q], acc)
+
+    acc2 = _loop2((0, BX), (0, BY), clamped, jnp.zeros((64, NZ), jnp.float32), unroll=4)
 
     for copy in set_b:
         copy.wait_recv()
     _loop2((BX + 2, BX + 3), (0, BY + 3), search, unroll=2)
     _loop2((0, BX + 2), (BY + 2, BY + 3), search, unroll=2)
     _apply(u_at, e_at, adder(image, lambda ex, x: False, 1, at_nodes), range(-1, BX), BY, 1, False)
-    if todo:
-        going = begin(0, todo.pop(0), finish(going))
     _apply(u_at, e_at, adder(image, lambda ex, x: False, 1, at_nodes), range(BX, BX + 1), -1, BY + 2, False, unroll=2)
 
     def edge(x, y, _):
@@ -515,65 +536,54 @@
     _loop2((BX, BX + 1), (0, BY + 1), edge, unroll=3)
     _loop2((0, BX), (BY, BY + 1), edge)
     if todo:
-        going = begin(0, todo.pop(0), finish(going))
+        going = begin1(todo.pop(0), finish(going))
 
     def q_at(k, pz, x, y, ct):
         return qm[k, pz, x, y, ct]
 
     _apply(q_at, e_at, adder(wf, lambda ex, x: x == ex + 1 or ex == 0, 0, at_nodes), range(BX), 0, BY, True, unroll=2)
-    if todo:
-        going = begin(0, todo.pop(0), finish(going))
 
     def second_gram(x, y, acc):
-        fr = free[x + 1, y + 1]
-        mine = jnp.where((x < BX) & (y < BY), 1.0, 0.0).astype(jnp.float32)
-        right = []
+        at = [(k, pz) for k in range(3) for pz in (0, 1)]
+        return pair([qm[k, pz, x, y] for k, pz in at], [wf[k, pz, x, y] for k, pz in at], acc)
+
+    acc2 = _loop2((0, BX + 1), (0, BY + 1), second_gram, acc2, unroll=3)
+    last = acc2[:24] + acc2[32:56]
+    last = last + pltpu.roll(last, 64, axis=1)
+    last = jnp.where(lane < 24, last, 0.0)
+    last = last[:8] + pltpu.roll(last[8:16], 24, axis=1) + pltpu.roll(last[16:], 48, axis=1)
+    n_going = begin2(0, last)
+    while todo:
+        going = begin1(todo.pop(0), finish(going))
+    n_todo = list(range(1, len(phases2)))
+    if n_todo:
+        n_going = begin2(n_todo.pop(0), finish(n_going))
+    table = finish(going)
+    tiles, scales = _eliminate(_system(table), jnp.zeros((1, NZ), jnp.float32), range(24))
+
+    def prepare(x, y, _):
         for k in range(3):
-            w = fr * _gather_z(wf[k, 0, x, y], wf[k, 1, x, y]) + (mine * (1.0 - fr)) * qf[k, x, y]
-            high, low = _split(jnp.concatenate([_rows(w), gap8], 0))
-            right.append(jnp.concatenate([high, gap32, low, gap32], 0))
-        left = jnp.concatenate([split[k, x, y] for k in range(3)], 1)
-        return acc + _nt(left, jnp.concatenate(right, 1))
-
-    acc2 = _loop2((0, BX + 1), (0, BY + 1), second_gram, jnp.zeros((96, NZ), jnp.float32), unroll=3)
-    last = acc2[24:48] + acc2[72:]
-    last = last + pltpu.roll(last, 64, axis=1)
-    n_going = begin(1, 0, last)
-    table = finish(going)
-    todo = list(range(1, len(phases)))
-    if todo:
-        n_going = begin(1, todo.pop(0), finish(n_going))
-    tiles, scales = _eliminate(_system(table), jnp.zeros((1, NZ), jnp.float32), range(24))
-    if todo:
-        n_going = begin(1, todo.pop(0), finish(n_going))
-
-    grid_y = j * BY - BY + lax.broadcasted_iota(jnp.int32, (3 * BY, NZ), 0)
-    ok_y = (grid_y >= 0) & (grid_y < ny * BY)
-
-    def present(p):
-        gx = i * BX + p - 2
-        return jnp.where(ok_y & (gx >= 0) & (gx < nx * BX), 1.0, 0.0).astype(jnp.float32)
-
-    def spread(p, v):
-        zsum[p, 0] = v
-        zsum[p, 1] = _shift(v, 1) + _shift(v, -1)
-        zsum[p, 2] = _shift(v, 2) + _shift(v, -2)
-
-    def near(p, dy, dz):
-        return zsum[p, dz, BY + dy : 2 * BY + dy]
+            for pz in (0, 1):
+                both = jnp.concatenate([_rows(masked[k, pz, x + 1, y + 1]), _rows(qm[k, pz, x, y])], 0)
+                split[k, x, y, :, pz * NZ : pz * NZ + NZ] = jnp.concatenate(_split(both), 0)
+        return 0
+
+    _loop2((0, BX + 1), (0, BY + 1), prepare)
+
+    def block(p, t):
+        return inside(BX * ((p - 2) // BX), BY * (t - 1))
 
     for p in range(BX + 4):
-        spread(p, present(p))
-    weights = _cone(near)
+        for t in range(3):
+            rim[p, BY * t : BY * t + BY] = jnp.zeros((BY, NZ), jnp.float32) + block(p, t)
+    weights = _cone(rim)
     rho = [0.3 + 0.7 * lev[2 + x, 2 : 2 + BY, 0, :].astype(jnp.float32) / (LEVELS - 1) for x in range(BX)]
 
-    if todo:
-        n_going = begin(1, todo.pop(0), finish(n_going))
     last = finish(n_going)
-    last = jnp.where(lane < 24, last, 0.0)
-    last = pltpu.roll(last, 24, axis=1)
+    lane8 = lax.broadcasted_iota(jnp.int32, (8, NZ), 1)
     for t in range(3):
-        tiles[3 + t] = tiles[3 + t] + last[8 * t : 8 * t + 8]
+        rows = last if t == 1 else pltpu.roll(last, (24 * (1 - t)) % NZ, axis=1)
+        tiles[3 + t] = tiles[3 + t] + jnp.where((lane8 >= 24) & (lane8 < 48), rows, 0.0)
     tiles, scales = _eliminate(tiles, scales, range(24, 48))
     half = jnp.concatenate(tiles[6:], 0) * scales
     mix = half + pltpu.roll(half, 48, axis=1)
@@ -582,13 +592,11 @@
     coefs = jnp.concatenate([high, low], 0)[:, :96]
 
     def combine(x, y, _):
-        fr = free[x + 1, y + 1]
         for k in range(3):
             u = jnp.dot(coefs, split[k, x, y], preferred_element_type=jnp.float32)
             u = u[:24] + u[32:56]
-            s, t = _sum_diff(fr * u.reshape(CT, 8, NZ))
-            disp[k, 0, x, y] = s
-            disp[k, 1, x, y] = t
+            for pz in (0, 1):
+                disp[k, pz, x, y] = u[:, pz * NZ : pz * NZ + NZ].reshape(CT, 8, NZ)
         return 0
 
     _loop2((0, BX + 1), (0, BY + 1), combine, unroll=3)
@@ -629,8 +637,9 @@
     for copy in group:
         copy.wait_recv()
     for p in range(BX + 4):
-        spread(p, jnp.where(present(p) > 0.0, vals[p], 0.0))
-    sums = _cone(near)
+        for t in range(3):
+            rim[p, BY * t : BY * t + BY] = vals[p, BY * t : BY * t + BY] * block(p, t)
+    sums = _cone(rim)
     for x in range(BX):
         out[x] = sums[x] / (rho[x] * weights[x])
     for copy in group:
@@ -638,23 +647,29 @@
 
 
 def _phases(nx, ny):
-    groups = [[(1, 0)], [(2, 0), (0, 1), (2, 1)]]
-    groups.append([(4 * o, 0) for o in range(1, nx // 4)])
-    groups.append([(0, 2 * o) for o in range(1, ny // 2)])
-    return [g for g in groups if g]
+    core, along_x = [(1, 0)], [(2, 0), (0, 1), (2, 1)]
+    along_y = [(4 * o, 0) for o in range(1, nx // 4)]
+    along_z = [(0, 2 * o) for o in range(1, ny // 2)]
+
+    def product(fast, slow):
+        return [(a ^ c, b ^ d) for c, d in [(0, 0)] + slow for a, b in [(0, 0)] + fast][1:]
+
+    first = [product(core, along_x), along_y, along_z]
+    second = [product(core, along_x), product(along_y, along_z)]
+    return [g for g in first if g], [g for g in second if g]
 
 
 def solution(mesh):
     nx, ny = mesh.shape["gx"], mesh.shape["gy"]
-    phases = _phases(nx, ny)
-    slots = sum(len(g) for g in phases)
+    phases, phases2 = _phases(nx, ny)
+    slots, slots2 = (sum(len(g) for g in p) for p in (phases, phases2))
     f32 = jnp.float32
     dma = pltpu.SemaphoreType.DMA
     any_space = pl.BlockSpec(memory_space=pl.ANY)
 
     def local(forces, levels, supports):
         return pl.pallas_call(
-            functools.partial(_kernel, nx, ny, phases),
+            functools.partial(_kernel, nx, ny, phases, phases2),
             out_shape=jax.ShapeDtypeStruct((BX, BY, NZ), f32),
             in_specs=[any_space] * 3,
             out_specs=pl.BlockSpec(memory_space=pltpu.VMEM),
@@ -673,16 +688,18 @@
                 pltpu.VMEM((3, BX + 1, BY + 1, CT, 8, NZ), f32),
                 pltpu.VMEM((3, 2, BX + 1, BY + 1, CT, 8, NZ), f32),
                 pltpu.VMEM((3, 2, BX + 1, BY + 1, CT, 8, NZ), f32),
-                pltpu.VMEM((3, BX + 1, BY + 1, 96, NZ), jnp.bfloat16),
+                pltpu.VMEM((3, BX + 1, BY + 1, 96, 2 * NZ), jnp.bfloat16),
                 pltpu.VMEM((3, 2, BX + 1, BY + 1, CT, 8, NZ), f32),
                 pltpu.VMEM((BX, BY, 8, NZ), f32),
                 pltpu.VMEM((BX + 4, 3 * BY, NZ), f32),
-                pltpu.VMEM((BX + 4, 3, 3 * BY, NZ), f32),
-                pltpu.VMEM((2 * len(phases), CASES, NZ), f32),
-                pltpu.VMEM((2 * slots, CASES, NZ), f32),
+                pltpu.VMEM((BX + 4, 3 * BY, NZ), f32),
+                pltpu.VMEM((len(phases), CASES, NZ), f32),
+                pltpu.VMEM((slots, CASES, NZ), f32),
+                pltpu.VMEM((len(phases2), 8, NZ), f32),
+                pltpu.VMEM((slots2, 8, NZ), f32),
                 dma((3,)),
                 dma((8,)), dma((8,)), dma((8,)), dma((8,)), dma((14,)), dma((14,)), dma((8,)), dma((8,)),
-                dma((2 * slots,)), dma((2 * slots,)),
+                dma((slots,)), dma((slots,)), dma((slots2,)), dma((slots2,)),
             ],
             compiler_params=pltpu.CompilerParams(collective_id=0, has_side_effects=True),
         )(

time: 68 us -> 58.7 us (0.86)
  Pallas kernels: 66.5 us -> 57.2 us
    pallas_call x1, Pallas kernels: 66.5 us -> 57.2 us  [local(): pl.pallas_call(functools.partial(_kernel, nx, ny, phases, phases2), out_s...]
where the time goes in v3:
time: 58.7 us; the launch traced here: 58.5 us
  Pallas kernels  57.2 us (97%)
  local copies, waits for them, and re-layouts  1.3 us (2%)
    pallas_call x1, Pallas kernels, local(): pl.pallas_call(functools.partial(_kernel, nx, ny, phases, phases2), out_s...  57.2 us
    unnamed x1, local copies, waits for them, and re-layouts  1.3 us

profile of v3, /device:TPU:1, one launch (start us, length us, event | category | flops | bytes accessed | tf_op | source)
XLA Modules:
  0.0 58.5 jit_solution(5760548041658805680)
XLA Ops:
  0.0 57.2 %shard_map.37 = f32[2,8,128]{2,1,0:T(8,128)} custom-call(f32[1152,128]{1,0:T(8,128)} %bitcast.3, s32[2,8,1,128]{3,2,1,0:T(1,128)} %bitcast.4, s32[2,8,1,128]{3,2,1,0:T(1,128)} %bitcast.5), custom_call_target="tpu_custom_call" | custom-call | tf_op jit(solution)/shard_map/pallas_call | solution.py:671
  57.2 1.3 %copy.5 = f32[2,8,128]{2,1,0:T(8,128)} copy(f32[2,8,128]{2,1,0:T(8,128)} %shard_map.37) | data formatting | bytes 16384

commit v4 on v3

--- a/solution.py
+++ b/solution.py
@@ -273,15 +273,31 @@
     return [b[8 * i : 8 * i + 8] for b in blocks for i in range(3)]
 
 
-def _eliminate(tiles, scales, steps):
-    lane = lax.broadcasted_iota(jnp.int32, (1, NZ), 1)
-    for j in steps:
-        row = tiles[j // 8][j % 8 : j % 8 + 1]
-        scale = 1.0 / row[:, j : j + 1]
-        factor = jnp.where(lane == j, 0.0, row * scale)
-        scales = jnp.where(lane == j, scale, scales)
-        for t in range((j + 1) // 8, 9):
-            tiles[t] = tiles[t] - tiles[t][:, j : j + 1] * factor
+def _eliminate(tiles, scales, steps, width=4):
+    lane = lax.broadcasted_iota(jnp.int32, (8, NZ), 1)
+
+    def one_row(x, r):
+        return jnp.broadcast_to(x[r : r + 1], (8, NZ))
+
+    for first in range(steps.start, steps.stop, width):
+        own, at = first // 8, first % 8
+        live = range(own, 9)
+        cols = [{t: jnp.broadcast_to(tiles[t][:, first + m : first + m + 1], (8, NZ)) for t in live} for m in range(width)]
+        rows = [one_row(tiles[own], at + m) for m in range(width)]
+        factors = []
+        for m in range(width):
+            scale = 1.0 / one_row(cols[m][own], at + m)
+            factor = jnp.where(lane == first + m, 0.0, rows[m] * scale)
+            scales = jnp.where(lane == first + m, scale, scales)
+            factors.append(factor)
+            for later in range(m + 1, width):
+                share = one_row(cols[later][own], at + m) * scale
+                rows[later] = rows[later] - one_row(cols[m][own], at + later) * factor
+                for t in live:
+                    cols[later][t] = cols[later][t] - cols[m][t] * share
+        for t in live:
+            for m in range(width):
+                tiles[t] = tiles[t] - cols[m][t] * factors[m]
     return tiles, scales
 
 
@@ -310,15 +326,18 @@
     return result
 
 
-SET_A = [(dx, dy, _span(dx, -1, 2, BX), _span(dy, -1, 8, BY)) for dx, dy in NEIGHBOURS]
-SET_B = [
-    (-1, 0, (1, 3, 1), (0, 0, BY)),
-    (0, -1, (0, 0, BX), (1, 9, 1)),
+EDGE_Y = [(0, dy, (0, 0, BX), _span(dy, -1, 8, BY)) for dy in (-1, 1)]
+EDGE_X = [(dx, 0, _span(dx, -1, 2, BX), (0, 0, BY)) for dx in (-1, 1)]
+CORNERS = [(dx, dy, _span(dx, -1, 2, BX), _span(dy, -1, 8, BY)) for dx in (-1, 1) for dy in (-1, 1)]
+FAR_Y = [(0, -1, (0, 0, BX), (1, 9, 1))]
+FAR_X = [(-1, 0, (1, 3, 1), (0, 0, BY))]
+FAR_CORNERS = [
     (-1, 1, (1, 3, 1), (7, -1, 1)),
     (-1, -1, (1, 3, 1), (0, 8, 2)),
     (-1, -1, (0, 2, 1), (1, 9, 1)),
     (1, -1, (1, -1, 1), (1, 9, 1)),
 ]
+HALO = [EDGE_Y, EDGE_X, CORNERS, FAR_Y, FAR_X, FAR_CORNERS]
 
 
 def _kernel(nx, ny, phases, phases2, forces, levels, supports, out, nat, lev, sup, stiff, stiffz, inv, free, field, dire, masked,
@@ -360,7 +379,7 @@
 
     pl.semaphore_wait(barrier, len(peers))
 
-    small, set_a, set_b = [], [], []
+    small = []
     for n, (dx, dy) in enumerate(NEIGHBOURS):
         (a, b, c), (d, e, f) = _span(dx, -2, 3, BX), _span(dy, -2, 9, BY)
         small.append(pltpu.make_async_remote_copy(
@@ -370,11 +389,26 @@
         small.append(pltpu.make_async_remote_copy(
             supports.at[a : a + c, d : d + f], sup.at[b + 1 : b + 1 + c, e + 1 : e + 1 + f],
             s_send.at[n], s_recv.at[n], device_id=there(dx, dy), device_id_type=MESH))
-    for n, (dx, dy, (a, b, c), (d, e, f)) in enumerate(SET_A + SET_B):
-        (set_a if n < len(SET_A) else set_b).append(pltpu.make_async_remote_copy(
-            field.at[:, a + 1 : a + 1 + c, d + 1 : d + 1 + f], field.at[:, b + 1 : b + 1 + c, e + 1 : e + 1 + f],
-            f_send.at[n], f_recv.at[n], device_id=there(dx, dy), device_id_type=MESH))
-    for copy in small + set_a + set_b:
+
+    odd = lax.rem(i, 2)
+    halo, n = [], 0
+    for group in HALO:
+        halo.append([])
+        for dx, dy, (a, b, c), (d, e, f) in group:
+            if dx and dy:
+                direct = odd if dx > 0 else 1 - odd
+                columns = pl.ds(e + 1 + direct * (d - e), f)
+                peer = there(dx, direct * dy)
+            else:
+                columns = pl.ds(d + 1, f)
+                peer = there(dx, dy)
+            halo[-1].append(pltpu.make_async_remote_copy(
+                field.at[:, a + 1 : a + 1 + c, columns], field.at[:, b + 1 : b + 1 + c, e + 1 : e + 1 + f],
+                f_send.at[n], f_recv.at[n], device_id=peer, device_id_type=MESH))
+            n += 1
+    edge_y, edge_x, corners, far_y, far_x, far_corners = halo
+    set_b = far_y + far_x + far_corners
+    for copy in small + edge_y + edge_x:
         copy.start()
     for copy in small:
         copy.wait_recv()
@@ -414,13 +448,11 @@
             masked[k, 1, x, y] = t
         return 0
 
-    _loop2((1, 1 + BX), (1, 1 + BY), search, unroll=2)
-    for copy in set_a:
+    for copy in edge_y:
         copy.wait_recv()
-    _loop2((0, 1), (0, BY + 2), search, unroll=2)
-    _loop2((BX + 1, BX + 2), (0, BY + 2), search, unroll=2)
-    for y in (0, BY + 1):
-        _loop2((1, 1 + BX), (y, y + 1), search)
+    for copy in corners + far_y + far_x:
+        copy.start()
+    _loop2((1, 1 + BX), (0, BY + 2), search, unroll=2)
 
     def u_at(k, pz, x, y, ct):
         return masked[k, pz, x + 1, y + 1, ct]
@@ -440,7 +472,17 @@
         return add
 
     at_nodes = range(BX + 1)
-    _apply(u_at, e_at, adder(image, lambda ex, x: x == ex + 1, 1, at_nodes), range(-1, BX), -1, BY + 1, True, unroll=3)
+    add_near = adder(image, lambda ex, x: ex == 0 or x == BX, 1, at_nodes)
+    _apply(u_at, e_at, add_near, range(0, 1), -1, BY + 1, True, unroll=3)
+    for copy in far_y:
+        copy.wait_recv()
+    for copy in far_corners:
+        copy.start()
+    for copy in edge_x + corners:
+        copy.wait_recv()
+    _loop2((0, 1), (0, BY + 2), search, unroll=2)
+    _loop2((BX + 1, BX + 2), (0, BY + 2), search, unroll=2)
+    _apply(u_at, e_at, add_near, (-1, BX - 1), -1, BY + 1, True, unroll=3)
 
     gap = jnp.zeros((16, NZ), jnp.bfloat16)
     gap8 = jnp.zeros((8, NZ), jnp.float32)
@@ -470,7 +512,7 @@
             right.append(jnp.concatenate([high, gap, low, gap], 0))
         return acc + _nt(jnp.concatenate(left, 1), jnp.concatenate(right, 1))
 
-    acc = _loop2((0, BX), (0, BY), first_gram, jnp.zeros((96, NZ), jnp.float32))
+    acc = _loop2((0, BX), (0, BY), first_gram, jnp.zeros((96, NZ), jnp.float32), unroll=4)
     lane = lax.broadcasted_iota(jnp.int32, (CASES, NZ), 1)
     both = acc[:48] + acc[48:]
     both = both + pltpu.roll(both, 64, axis=1)
@@ -522,7 +564,7 @@
 
     acc2 = _loop2((0, BX), (0, BY), clamped, jnp.zeros((64, NZ), jnp.float32), unroll=4)
 
-    for copy in set_b:
+    for copy in far_x + far_corners:
         copy.wait_recv()
     _loop2((BX + 2, BX + 3), (0, BY + 3), search, unroll=2)
     _loop2((0, BX + 2), (BY + 2, BY + 3), search, unroll=2)
@@ -559,7 +601,7 @@
     if n_todo:
         n_going = begin2(n_todo.pop(0), finish(n_going))
     table = finish(going)
-    tiles, scales = _eliminate(_system(table), jnp.zeros((1, NZ), jnp.float32), range(24))
+    tiles, scales = _eliminate(_system(table), jnp.zeros((8, NZ), jnp.float32), range(24))
 
     def prepare(x, y, _):
         for k in range(3):
@@ -568,7 +610,7 @@
                 split[k, x, y, :, pz * NZ : pz * NZ + NZ] = jnp.concatenate(_split(both), 0)
         return 0
 
-    _loop2((0, BX + 1), (0, BY + 1), prepare)
+    _loop2((0, BX + 1), (0, BY + 1), prepare, unroll=3)
 
     def block(p, t):
         return inside(BX * ((p - 2) // BX), BY * (t - 1))
@@ -585,7 +627,7 @@
         rows = last if t == 1 else pltpu.roll(last, (24 * (1 - t)) % NZ, axis=1)
         tiles[3 + t] = tiles[3 + t] + jnp.where((lane8 >= 24) & (lane8 < 48), rows, 0.0)
     tiles, scales = _eliminate(tiles, scales, range(24, 48))
-    half = jnp.concatenate(tiles[6:], 0) * scales
+    half = jnp.concatenate([t * scales for t in tiles[6:]], 0)
     mix = half + pltpu.roll(half, 48, axis=1)
     mix = jnp.concatenate([mix, gap8], 0)
     high, low = _split(mix)
@@ -632,7 +674,7 @@
             device_id=there(dx, dy), device_id_type=MESH))
     for copy in group:
         copy.start()
-    for copy in small + set_a + set_b + sent:
+    for copy in small + edge_y + edge_x + corners + set_b + sent:
         copy.wait_send()
     for copy in group:
         copy.wait_recv()

time: 58.7 us -> 57.1 us (0.973)
  Pallas kernels: 57.2 us -> 55.7 us
    pallas_call x1, Pallas kernels: 57.2 us -> 55.7 us  [local(): pl.pallas_call(functools.partial(_kernel, nx, ny, phases, phases2), out_s...]
where the time goes in v4:
time: 57.1 us; the launch traced here: 57 us
  Pallas kernels  55.7 us (98%)
  local copies, waits for them, and re-layouts  1.3 us (2%)
    pallas_call x1, Pallas kernels, local(): pl.pallas_call(functools.partial(_kernel, nx, ny, phases, phases2), out_s...  55.7 us
    unnamed x1, local copies, waits for them, and re-layouts  1.3 us

profile of v4, /device:TPU:1, one launch (start us, length us, event | category | flops | bytes accessed | tf_op | source)
XLA Modules:
  0.0 57.0 jit_solution(4802305953933789031)
XLA Ops:
  0.0 55.7 %shard_map.37 = f32[2,8,128]{2,1,0:T(8,128)} custom-call(f32[1152,128]{1,0:T(8,128)} %bitcast.3, s32[2,8,1,128]{3,2,1,0:T(1,128)} %bitcast.4, s32[2,8,1,128]{3,2,1,0:T(1,128)} %bitcast.5), custom_call_target="tpu_custom_call" | custom-call | tf_op jit(solution)/shard_map/pallas_call | solution.py:713
  55.7 1.3 %copy.5 = f32[2,8,128]{2,1,0:T(8,128)} copy(f32[2,8,128]{2,1,0:T(8,128)} %shard_map.37) | data formatting | bytes 16384

commit v5 on v4

--- a/solution.py
+++ b/solution.py
@@ -267,7 +267,7 @@
 
     blocks = [
         join(table, left(table, 24)),
-        join(left(table, 48), jnp.zeros_like(table)),
+        join(left(table, 48), left(table, 72)),
         join(left(table, 24), left(table, 48)),
     ]
     return [b[8 * i : 8 * i + 8] for b in blocks for i in range(3)]
@@ -341,7 +341,7 @@
 
 
 def _kernel(nx, ny, phases, phases2, forces, levels, supports, out, nat, lev, sup, stiff, stiffz, inv, free, field, dire, masked,
-            image, qf, qm, wf, split, disp, energy, vals, rim, gram_send, gram_recv, last_send, last_recv, local_sem, l_send, l_recv, s_send,
+            image, qm, wf, split, disp, energy, vals, rim, gram_send, gram_recv, last_send, last_recv, local_sem, l_send, l_recv, s_send,
             s_recv, f_send, f_recv, v_send, v_recv, g_send, g_recv, n_send, n_recv):
     i, j = lax.axis_index("gx"), lax.axis_index("gy")
 
@@ -408,7 +408,7 @@
             n += 1
     edge_y, edge_x, corners, far_y, far_x, far_corners = halo
     set_b = far_y + far_x + far_corners
-    for copy in small + edge_y + edge_x:
+    for copy in small + edge_y + far_y + edge_x:
         copy.start()
     for copy in small:
         copy.wait_recv()
@@ -448,11 +448,11 @@
             masked[k, 1, x, y] = t
         return 0
 
-    for copy in edge_y:
+    for copy in edge_y + far_y:
         copy.wait_recv()
-    for copy in corners + far_y + far_x:
+    for copy in corners + far_corners + far_x:
         copy.start()
-    _loop2((1, 1 + BX), (0, BY + 2), search, unroll=2)
+    _loop2((1, 1 + BX), (0, BY + 3), search, unroll=2)
 
     def u_at(k, pz, x, y, ct):
         return masked[k, pz, x + 1, y + 1, ct]
@@ -474,17 +474,12 @@
     at_nodes = range(BX + 1)
     add_near = adder(image, lambda ex, x: ex == 0 or x == BX, 1, at_nodes)
     _apply(u_at, e_at, add_near, range(0, 1), -1, BY + 1, True, unroll=3)
-    for copy in far_y:
-        copy.wait_recv()
-    for copy in far_corners:
-        copy.start()
     for copy in edge_x + corners:
         copy.wait_recv()
     _loop2((0, 1), (0, BY + 2), search, unroll=2)
     _loop2((BX + 1, BX + 2), (0, BY + 2), search, unroll=2)
     _apply(u_at, e_at, add_near, (-1, BX - 1), -1, BY + 1, True, unroll=3)
 
-    gap = jnp.zeros((16, NZ), jnp.bfloat16)
     gap8 = jnp.zeros((8, NZ), jnp.float32)
     gap32 = jnp.zeros((32, NZ), jnp.bfloat16)
 
@@ -505,18 +500,20 @@
         nodes, fr = above(x, y)
         left, right = [], []
         for k, (d, im, q) in enumerate(nodes):
-            qf[k, x, y] = q
             r0 = LOAD * fr * field[k, x + 1, y + 1]
+            held = jnp.concatenate([_rows((1.0 - fr) * q), gap8], 0).astype(jnp.bfloat16)
             left.append(jnp.concatenate(_split(jnp.concatenate([_rows(d), _rows(q)], 0)), 0))
             high, low = _split(jnp.concatenate([_rows(im), _rows(r0)], 0))
-            right.append(jnp.concatenate([high, gap, low, gap], 0))
+            right.append(jnp.concatenate([high, held[:16], low, held[16:]], 0))
         return acc + _nt(jnp.concatenate(left, 1), jnp.concatenate(right, 1))
 
     acc = _loop2((0, BX), (0, BY), first_gram, jnp.zeros((96, NZ), jnp.float32), unroll=4)
     lane = lax.broadcasted_iota(jnp.int32, (CASES, NZ), 1)
     both = acc[:48] + acc[48:]
+    held = both[24:]
+    held = jnp.where(lane < 112, pltpu.roll(held, 48, axis=1), held)
     both = both + pltpu.roll(both, 64, axis=1)
-    table = jnp.where(lane < 48, both[:24], jnp.where(lane < 96, pltpu.roll(both[24:], 48, axis=1), 0.0))
+    table = jnp.where(lane < 48, both[:24], jnp.where(lane < 96, pltpu.roll(both[24:], 48, axis=1), held))
 
     sent = []
 
@@ -557,17 +554,11 @@
             b.append(jnp.concatenate([high, gap32, low, gap32], 0))
         return acc + _nt(jnp.concatenate(a, 1), jnp.concatenate(b, 1))
 
-    def clamped(x, y, acc):
-        fr = free[x + 1, y + 1]
-        q = [qf[k, x, y] for k in range(3)]
-        return pair(q, [(1.0 - fr) * v for v in q], acc)
-
-    acc2 = _loop2((0, BX), (0, BY), clamped, jnp.zeros((64, NZ), jnp.float32), unroll=4)
-
     for copy in far_x + far_corners:
         copy.wait_recv()
     _loop2((BX + 2, BX + 3), (0, BY + 3), search, unroll=2)
-    _loop2((0, BX + 2), (BY + 2, BY + 3), search, unroll=2)
+    _loop2((0, 1), (BY + 2, BY + 3), search)
+    _loop2((BX + 1, BX + 2), (BY + 2, BY + 3), search)
     _apply(u_at, e_at, adder(image, lambda ex, x: False, 1, at_nodes), range(-1, BX), BY, 1, False)
     _apply(u_at, e_at, adder(image, lambda ex, x: False, 1, at_nodes), range(BX, BX + 1), -1, BY + 2, False, unroll=2)
 
@@ -577,19 +568,19 @@
 
     _loop2((BX, BX + 1), (0, BY + 1), edge, unroll=3)
     _loop2((0, BX), (BY, BY + 1), edge)
+
+    def q_at(k, pz, x, y, ct):
+        return qm[k, pz, x, y, ct]
+
+    _apply(q_at, e_at, adder(wf, lambda ex, x: x == ex + 1 or ex == 0, 0, at_nodes), range(BX), 0, BY, True, unroll=2)
     if todo:
         going = begin1(todo.pop(0), finish(going))
-
-    def q_at(k, pz, x, y, ct):
-        return qm[k, pz, x, y, ct]
-
-    _apply(q_at, e_at, adder(wf, lambda ex, x: x == ex + 1 or ex == 0, 0, at_nodes), range(BX), 0, BY, True, unroll=2)
 
     def second_gram(x, y, acc):
         at = [(k, pz) for k in range(3) for pz in (0, 1)]
         return pair([qm[k, pz, x, y] for k, pz in at], [wf[k, pz, x, y] for k, pz in at], acc)
 
-    acc2 = _loop2((0, BX + 1), (0, BY + 1), second_gram, acc2, unroll=3)
+    acc2 = _loop2((0, BX + 1), (0, BY + 1), second_gram, jnp.zeros((64, NZ), jnp.float32), unroll=3)
     last = acc2[:24] + acc2[32:56]
     last = last + pltpu.roll(last, 64, axis=1)
     last = jnp.where(lane < 24, last, 0.0)
@@ -597,20 +588,21 @@
     n_going = begin2(0, last)
     while todo:
         going = begin1(todo.pop(0), finish(going))
+
+    def prepare(x, y, _):
+        for k in range(3):
+            for pz in (0, 1):
+                both = jnp.concatenate([_rows(masked[k, pz, x + 1, y + 1]), _rows(qm[k, pz, x, y])], 0)
+                split[k, x, y, :, pz * NZ : pz * NZ + NZ] = jnp.concatenate(_split(both), 0)
+        return 0
+
+    _loop2((0, BX + 1), (0, BY + 1), prepare, unroll=3)
+
     n_todo = list(range(1, len(phases2)))
     if n_todo:
         n_going = begin2(n_todo.pop(0), finish(n_going))
     table = finish(going)
     tiles, scales = _eliminate(_system(table), jnp.zeros((8, NZ), jnp.float32), range(24))
-
-    def prepare(x, y, _):
-        for k in range(3):
-            for pz in (0, 1):
-                both = jnp.concatenate([_rows(masked[k, pz, x + 1, y + 1]), _rows(qm[k, pz, x, y])], 0)
-                split[k, x, y, :, pz * NZ : pz * NZ + NZ] = jnp.concatenate(_split(both), 0)
-        return 0
-
-    _loop2((0, BX + 1), (0, BY + 1), prepare, unroll=3)
 
     def block(p, t):
         return inside(BX * ((p - 2) // BX), BY * (t - 1))
@@ -641,7 +633,7 @@
                 disp[k, pz, x, y] = u[:, pz * NZ : pz * NZ + NZ].reshape(CT, 8, NZ)
         return 0
 
-    _loop2((0, BX + 1), (0, BY + 1), combine, unroll=3)
+    _loop2((0, BX + 1), (0, BY + 1), combine, unroll=9)
 
     def s_at(k, pz, x, y, ct):
         return disp[k, pz, x, y, ct]
@@ -727,7 +719,6 @@
                 pltpu.VMEM((3, BX + 3, BY + 3, CT, 8, NZ), f32),
                 pltpu.VMEM((3, 2, BX + 3, BY + 3, CT, 8, NZ), f32),
                 pltpu.VMEM((3, 2, BX + 1, BY + 2, CT, 8, NZ), f32),
-                pltpu.VMEM((3, BX + 1, BY + 1, CT, 8, NZ), f32),
                 pltpu.VMEM((3, 2, BX + 1, BY + 1, CT, 8, NZ), f32),
                 pltpu.VMEM((3, 2, BX + 1, BY + 1, CT, 8, NZ), f32),
                 pltpu.VMEM((3, BX + 1, BY + 1, 96, 2 * NZ), jnp.bfloat16),

time: 57.1 us -> 58.3 us (1.021)
  Pallas kernels: 55.7 us -> 56.8 us
    pallas_call x1, Pallas kernels: 55.7 us -> 56.8 us  [local(): pl.pallas_call(functools.partial(_kernel, nx, ny, phases, phases2), out_s...]
where the time goes in v5:
time: 58.3 us; the launch traced here: 58.1 us
  Pallas kernels  56.8 us (97%)
  local copies, waits for them, and re-layouts  1.3 us (2%)
    pallas_call x1, Pallas kernels, local(): pl.pallas_call(functools.partial(_kernel, nx, ny, phases, phases2), out_s...  56.8 us
    unnamed x1, local copies, waits for them, and re-layouts  1.3 us

profile of v5, /device:TPU:1, one launch (start us, length us, event | category | flops | bytes accessed | tf_op | source)
XLA Modules:
  0.0 58.1 jit_solution(5863948137951831094)
XLA Ops:
  0.0 56.8 %shard_map.37 = f32[2,8,128]{2,1,0:T(8,128)} custom-call(f32[1152,128]{1,0:T(8,128)} %bitcast.3, s32[2,8,1,128]{3,2,1,0:T(1,128)} %bitcast.4, s32[2,8,1,128]{3,2,1,0:T(1,128)} %bitcast.5), custom_call_target="tpu_custom_call" | custom-call | tf_op jit(solution)/shard_map/pallas_call | solution.py:705
  56.8 1.3 %copy.5 = f32[2,8,128]{2,1,0:T(8,128)} copy(f32[2,8,128]{2,1,0:T(8,128)} %shard_map.37) | data formatting | bytes 16384

commit v6 on v5

--- a/solution.py
+++ b/solution.py
@@ -326,18 +326,15 @@
     return result
 
 
-EDGE_Y = [(0, dy, (0, 0, BX), _span(dy, -1, 8, BY)) for dy in (-1, 1)]
-EDGE_X = [(dx, 0, _span(dx, -1, 2, BX), (0, 0, BY)) for dx in (-1, 1)]
-CORNERS = [(dx, dy, _span(dx, -1, 2, BX), _span(dy, -1, 8, BY)) for dx in (-1, 1) for dy in (-1, 1)]
-FAR_Y = [(0, -1, (0, 0, BX), (1, 9, 1))]
-FAR_X = [(-1, 0, (1, 3, 1), (0, 0, BY))]
-FAR_CORNERS = [
+SET_A = [(dx, dy, _span(dx, -1, 2, BX), _span(dy, -1, 8, BY)) for dx, dy in NEIGHBOURS]
+SET_B = [
+    (-1, 0, (1, 3, 1), (0, 0, BY)),
+    (0, -1, (0, 0, BX), (1, 9, 1)),
     (-1, 1, (1, 3, 1), (7, -1, 1)),
     (-1, -1, (1, 3, 1), (0, 8, 2)),
     (-1, -1, (0, 2, 1), (1, 9, 1)),
     (1, -1, (1, -1, 1), (1, 9, 1)),
 ]
-HALO = [EDGE_Y, EDGE_X, CORNERS, FAR_Y, FAR_X, FAR_CORNERS]
 
 
 def _kernel(nx, ny, phases, phases2, forces, levels, supports, out, nat, lev, sup, stiff, stiffz, inv, free, field, dire, masked,
@@ -390,25 +387,15 @@
             supports.at[a : a + c, d : d + f], sup.at[b + 1 : b + 1 + c, e + 1 : e + 1 + f],
             s_send.at[n], s_recv.at[n], device_id=there(dx, dy), device_id_type=MESH))
 
-    odd = lax.rem(i, 2)
-    halo, n = [], 0
-    for group in HALO:
-        halo.append([])
-        for dx, dy, (a, b, c), (d, e, f) in group:
-            if dx and dy:
-                direct = odd if dx > 0 else 1 - odd
-                columns = pl.ds(e + 1 + direct * (d - e), f)
-                peer = there(dx, direct * dy)
-            else:
-                columns = pl.ds(d + 1, f)
-                peer = there(dx, dy)
-            halo[-1].append(pltpu.make_async_remote_copy(
-                field.at[:, a + 1 : a + 1 + c, columns], field.at[:, b + 1 : b + 1 + c, e + 1 : e + 1 + f],
-                f_send.at[n], f_recv.at[n], device_id=peer, device_id_type=MESH))
-            n += 1
-    edge_y, edge_x, corners, far_y, far_x, far_corners = halo
-    set_b = far_y + far_x + far_corners
-    for copy in small + edge_y + far_y + edge_x:
+    halo = []
+    for n, (dx, dy, (a, b, c), (d, e, f)) in enumerate(SET_A + SET_B):
+        halo.append(pltpu.make_async_remote_copy(
+            field.at[:, a + 1 : a + 1 + c, d + 1 : d + 1 + f], field.at[:, b + 1 : b + 1 + c, e + 1 : e + 1 + f],
+            f_send.at[n], f_recv.at[n], device_id=there(dx, dy), device_id_type=MESH))
+    near, far = halo[: len(SET_A)], halo[len(SET_A) :]
+    edge_y = [copy for copy, (dx, _, _, _) in zip(near, SET_A) if dx == 0]
+    edge_x = [copy for copy, (dx, _, _, _) in zip(near, SET_A) if dx != 0]
+    for copy in small + near + far:
         copy.start()
     for copy in small:
         copy.wait_recv()
@@ -448,11 +435,9 @@
             masked[k, 1, x, y] = t
         return 0
 
-    for copy in edge_y + far_y:
+    for copy in edge_y:
         copy.wait_recv()
-    for copy in corners + far_corners + far_x:
-        copy.start()
-    _loop2((1, 1 + BX), (0, BY + 3), search, unroll=2)
+    _loop2((1, 1 + BX), (0, BY + 2), search, unroll=2)
 
     def u_at(k, pz, x, y, ct):
         return masked[k, pz, x + 1, y + 1, ct]
@@ -474,7 +459,7 @@
     at_nodes = range(BX + 1)
     add_near = adder(image, lambda ex, x: ex == 0 or x == BX, 1, at_nodes)
     _apply(u_at, e_at, add_near, range(0, 1), -1, BY + 1, True, unroll=3)
-    for copy in edge_x + corners:
+    for copy in edge_x:
         copy.wait_recv()
     _loop2((0, 1), (0, BY + 2), search, unroll=2)
     _loop2((BX + 1, BX + 2), (0, BY + 2), search, unroll=2)
@@ -554,11 +539,10 @@
             b.append(jnp.concatenate([high, gap32, low, gap32], 0))
         return acc + _nt(jnp.concatenate(a, 1), jnp.concatenate(b, 1))
 
-    for copy in far_x + far_corners:
+    for copy in far:
         copy.wait_recv()
     _loop2((BX + 2, BX + 3), (0, BY + 3), search, unroll=2)
-    _loop2((0, 1), (BY + 2, BY + 3), search)
-    _loop2((BX + 1, BX + 2), (BY + 2, BY + 3), search)
+    _loop2((0, BX + 2), (BY + 2, BY + 3), search)
     _apply(u_at, e_at, adder(image, lambda ex, x: False, 1, at_nodes), range(-1, BX), BY, 1, False)
     _apply(u_at, e_at, adder(image, lambda ex, x: False, 1, at_nodes), range(BX, BX + 1), -1, BY + 2, False, unroll=2)
 
@@ -666,7 +650,7 @@
             device_id=there(dx, dy), device_id_type=MESH))
     for copy in group:
         copy.start()
-    for copy in small + edge_y + edge_x + corners + set_b + sent:
+    for copy in small + near + far + sent:
         copy.wait_send()
     for copy in group:
         copy.wait_recv()

time: 58.3 us -> 54.5 us (0.935)
  Pallas kernels: 56.8 us -> 53 us
    pallas_call x1, Pallas kernels: 56.8 us -> 53 us  [local(): pl.pallas_call(functools.partial(_kernel, nx, ny, phases, phases2), out_s...]
where the time goes in v6:
time: 54.5 us; the launch traced here: 54.3 us
  Pallas kernels  53 us (97%)
  local copies, waits for them, and re-layouts  1.3 us (2%)
    pallas_call x1, Pallas kernels, local(): pl.pallas_call(functools.partial(_kernel, nx, ny, phases, phases2), out_s...  53 us
    unnamed x1, local copies, waits for them, and re-layouts  1.3 us

profile of v6, /device:TPU:1, one launch (start us, length us, event | category | flops | bytes accessed | tf_op | source)
XLA Modules:
  0.0 54.3 jit_solution(5498502023753476591)
XLA Ops:
  0.0 53.0 %shard_map.37 = f32[2,8,128]{2,1,0:T(8,128)} custom-call(f32[1152,128]{1,0:T(8,128)} %bitcast.3, s32[2,8,1,128]{3,2,1,0:T(1,128)} %bitcast.4, s32[2,8,1,128]{3,2,1,0:T(1,128)} %bitcast.5), custom_call_target="tpu_custom_call" | custom-call | tf_op jit(solution)/shard_map/pallas_call | solution.py:689
  53.0 1.3 %copy.5 = f32[2,8,128]{2,1,0:T(8,128)} copy(f32[2,8,128]{2,1,0:T(8,128)} %shard_map.37) | data formatting | bytes 16384

commit v7 on v6

--- a/solution.py
+++ b/solution.py
@@ -541,8 +541,9 @@
 
     for copy in far:
         copy.wait_recv()
-    _loop2((BX + 2, BX + 3), (0, BY + 3), search, unroll=2)
-    _loop2((0, BX + 2), (BY + 2, BY + 3), search)
+    _loop2((BX + 2, BX + 3), (0, BY + 3), search, unroll=BY + 3)
+    for x in range(BX + 2):
+        search(x, BY + 2, 0)
     _apply(u_at, e_at, adder(image, lambda ex, x: False, 1, at_nodes), range(-1, BX), BY, 1, False)
     _apply(u_at, e_at, adder(image, lambda ex, x: False, 1, at_nodes), range(BX, BX + 1), -1, BY + 2, False, unroll=2)
 
@@ -550,8 +551,9 @@
         above(x, y)
         return 0
 
-    _loop2((BX, BX + 1), (0, BY + 1), edge, unroll=3)
-    _loop2((0, BX), (BY, BY + 1), edge)
+    _loop2((BX, BX + 1), (0, BY + 1), edge, unroll=BY + 1)
+    for x in range(BX):
+        edge(x, BY, 0)
 
     def q_at(k, pz, x, y, ct):
         return qm[k, pz, x, y, ct]
@@ -564,7 +566,7 @@
         at = [(k, pz) for k in range(3) for pz in (0, 1)]
         return pair([qm[k, pz, x, y] for k, pz in at], [wf[k, pz, x, y] for k, pz in at], acc)
 
-    acc2 = _loop2((0, BX + 1), (0, BY + 1), second_gram, jnp.zeros((64, NZ), jnp.float32), unroll=3)
+    acc2 = _loop2((0, BX + 1), (0, BY + 1), second_gram, jnp.zeros((64, NZ), jnp.float32), unroll=9)
     last = acc2[:24] + acc2[32:56]
     last = last + pltpu.roll(last, 64, axis=1)
     last = jnp.where(lane < 24, last, 0.0)

time: 54.5 us -> 53.2 us (0.976)
  Pallas kernels: 53 us -> 51.8 us
    pallas_call x1, Pallas kernels: 53 us -> 51.8 us  [local(): pl.pallas_call(functools.partial(_kernel, nx, ny, phases, phases2), out_s...]
where the time goes in v7:
time: 53.2 us; the launch traced here: 53.1 us
  Pallas kernels  51.8 us (97%)
  local copies, waits for them, and re-layouts  1.3 us (2%)
    pallas_call x1, Pallas kernels, local(): pl.pallas_call(functools.partial(_kernel, nx, ny, phases, phases2), out_s...  51.8 us
    unnamed x1, local copies, waits for them, and re-layouts  1.3 us

profile of v7, /device:TPU:1, one launch (start us, length us, event | category | flops | bytes accessed | tf_op | source)
XLA Modules:
  0.0 53.1 jit_solution(7795409168864279402)
XLA Ops:
  0.0 51.8 %shard_map.37 = f32[2,8,128]{2,1,0:T(8,128)} custom-call(f32[1152,128]{1,0:T(8,128)} %bitcast.3, s32[2,8,1,128]{3,2,1,0:T(1,128)} %bitcast.4, s32[2,8,1,128]{3,2,1,0:T(1,128)} %bitcast.5), custom_call_target="tpu_custom_call" | custom-call | tf_op jit(solution)/shard_map/pallas_call | solution.py:691
  51.8 1.3 %copy.5 = f32[2,8,128]{2,1,0:T(8,128)} copy(f32[2,8,128]{2,1,0:T(8,128)} %shard_map.37) | data formatting | bytes 16384

commit v8 on v7

--- a/solution.py
+++ b/solution.py
@@ -235,11 +235,11 @@
     return (s - d) + _shift(s + d, -1)
 
 
-def _loop2(xs, ys, body, state=0, unroll=1):
+def _loop2(xs, ys, body, state=0, unroll=1, planes=1):
     def outer(x, state):
         return lax.fori_loop(ys[0], ys[1], lambda y, st: body(x, y, st), state, unroll=unroll)
 
-    return lax.fori_loop(xs[0], xs[1], outer, state)
+    return lax.fori_loop(xs[0], xs[1], outer, state, unroll=planes)
 
 
 def _split(x):
@@ -566,7 +566,7 @@
         at = [(k, pz) for k in range(3) for pz in (0, 1)]
         return pair([qm[k, pz, x, y] for k, pz in at], [wf[k, pz, x, y] for k, pz in at], acc)
 
-    acc2 = _loop2((0, BX + 1), (0, BY + 1), second_gram, jnp.zeros((64, NZ), jnp.float32), unroll=9)
+    acc2 = _loop2((0, BX + 1), (0, BY + 1), second_gram, jnp.zeros((64, NZ), jnp.float32), unroll=9, planes=3)
     last = acc2[:24] + acc2[32:56]
     last = last + pltpu.roll(last, 64, axis=1)
     last = jnp.where(lane < 24, last, 0.0)
@@ -619,7 +619,7 @@
                 disp[k, pz, x, y] = u[:, pz * NZ : pz * NZ + NZ].reshape(CT, 8, NZ)
         return 0
 
-    _loop2((0, BX + 1), (0, BY + 1), combine, unroll=9)
+    _loop2((0, BX + 1), (0, BY + 1), combine, unroll=9, planes=3)
 
     def s_at(k, pz, x, y, ct):
         return disp[k, pz, x, y, ct]

time: 53.2 us -> 53.6 us (level)
  no operation moved by 1% of the time
where the time goes in v8:
time: 53.6 us; the launch traced here: 53.5 us
  Pallas kernels  52.2 us (97%)
  local copies, waits for them, and re-layouts  1.3 us (2%)
    pallas_call x1, Pallas kernels, local(): pl.pallas_call(functools.partial(_kernel, nx, ny, phases, phases2), out_s...  52.2 us
    unnamed x1, local copies, waits for them, and re-layouts  1.3 us

profile of v8, /device:TPU:1, one launch (start us, length us, event | category | flops | bytes accessed | tf_op | source)
XLA Modules:
  0.0 53.5 jit_solution(16738386609863780093)
XLA Ops:
  0.0 52.2 %shard_map.37 = f32[2,8,128]{2,1,0:T(8,128)} custom-call(f32[1152,128]{1,0:T(8,128)} %bitcast.3, s32[2,8,1,128]{3,2,1,0:T(1,128)} %bitcast.4, s32[2,8,1,128]{3,2,1,0:T(1,128)} %bitcast.5), custom_call_target="tpu_custom_call" | custom-call | tf_op jit(solution)/shard_map/pallas_call | solution.py:691
  52.2 1.3 %copy.5 = f32[2,8,128]{2,1,0:T(8,128)} copy(f32[2,8,128]{2,1,0:T(8,128)} %shard_map.37) | data formatting | bytes 16384
